TPU v7x, 32 devices: a whole 2x2x4 slice. The times are simulated.
32 devices in a mesh: pipe: 2 (over x), expert: 16 (over z, y, core).
Axes of the slice: x: 2, y: 2, z: 4, core: 2. Of those that a mesh axis runs over, the one named last changes fastest.
Arguments:
- tokens: bfloat16 [2, 2048, 7168], P('pipe', 'expert'), may hold values from -24 to 24
- grad_out: bfloat16 [2, 2048, 7168], P('pipe', 'expert'), may hold values from -6 to 6
- norm_gain: float32 [2, 7168], P('pipe'), may hold values from 0.25 to 1.75
- expert_ids: int32 [2, 2048, 2], P('pipe', 'expert'), may hold values from 0 to 3, all different within a row; in each aligned block of 128 rows (0 to 127, 128 to 255, ..., all dimensions but the last counted through in order) at most 80 rows name the same one
- gate_weights: float32 [2, 2048, 2], P('pipe', 'expert'), may hold values from 0.2 to 1
- w_gate: bfloat16 [2, 7168, 4096], P('pipe', None, 'expert'), may hold values from -0.0625 to 0.0625
- w_up: bfloat16 [2, 7168, 4096], P('pipe', None, 'expert'), may hold values from -0.0625 to 0.0625
- w_down: bfloat16 [2, 4096, 7168], P('pipe', 'expert'), may hold values from -0.1875 to 0.1875
Outputs:
- next_in: bfloat16 [2, 2048, 7168], P('pipe', 'expert')
- prev_grad: bfloat16 [2, 2048, 7168], P('pipe', 'expert')
Inputs may be any that keep to these rules, and one draw needn't show every extreme that they name: `expert_ids`: each token's 2 ids differ. In the rows of one device (aligned blocks of 128 rows of each section) no expert is named by more than 80 rows.
All inputs are finite; a program needn't handle non-finite values.
Results may differ from a plain program's by a relative error of at most 0.0048.
Values may be sent and summed in bfloat16 or wider, within the bound.
A program may use at most 192 MiB of HBM per device.

v0:
```python
from functools import partial

import jax
import jax.numpy as jnp
from jax import lax
from jax.sharding import PartitionSpec as P

SLICES = 4


EPSILON = 1e-06


def shifted(value, axis, steps):
    count = lax.axis_size(axis)
    pairs = [(source, (source + steps) % count) for source in range(count)]
    return lax.ppermute(value, axis, pairs)


def transpose_dot(left_arr, right_arr):
    return lax.dot_general(
        left_arr, right_arr, (((1,), (1,)), ((), ())), preferred_element_type=jnp.float32
    )


def expert_apply(rows_in, rows_grad, gate_cols, up_cols, down_rows):
    gate_pre = jnp.dot(rows_in, gate_cols, preferred_element_type=jnp.float32)
    up_pre = jnp.dot(rows_in, up_cols, preferred_element_type=jnp.float32)
    sigmoid_gate = jax.nn.sigmoid(gate_pre)
    swish_gate = gate_pre * sigmoid_gate
    hidden = (swish_gate * up_pre).astype(jnp.bfloat16)
    part_out = jnp.dot(hidden, down_rows, preferred_element_type=jnp.float32).astype(jnp.bfloat16)
    grad_hidden = transpose_dot(rows_grad, down_rows)
    grad_gate = (
        grad_hidden * up_pre * sigmoid_gate * (1.0 + gate_pre * (1.0 - sigmoid_gate))
    ).astype(jnp.bfloat16)
    grad_up = (grad_hidden * swish_gate).astype(jnp.bfloat16)
    part_grad = (transpose_dot(grad_gate, gate_cols) + transpose_dot(grad_up, up_cols)).astype(
        jnp.bfloat16
    )
    return (part_out, part_grad)


def body(tokens, grad_out, norm_gain, expert_ids, gate_weights, w_gate, w_up, w_down):
    tokens = tokens[0]
    grad_rows = grad_out[0]
    gain_wide = norm_gain[0][None, :]
    route_ids = expert_ids[0]
    route_weights = gate_weights[0]
    token_count, feature_width = tokens.shape
    top_count = route_ids.shape[1]
    devices = lax.axis_size("expert")
    experts = devices // SLICES
    step_size = 4 * experts * SLICES
    capacity = min(
        token_count, SLICES * ((token_count * top_count * 5 + step_size - 1) // step_size)
    )
    slot_count = experts * capacity
    run_rows = partial(expert_apply, gate_cols=w_gate[0], up_cols=w_up[0], down_rows=w_down[0])
    values = tokens.astype(jnp.float32)
    inverse = lax.rsqrt(jnp.mean(values * values, axis=-1, keepdims=True) + EPSILON)
    normed = (values * inverse * gain_wide).astype(jnp.bfloat16)
    flat_ids = route_ids.reshape(-1)
    onehot = (flat_ids[:, None] == jnp.arange(experts, dtype=jnp.int32)[None, :]).astype(jnp.int32)
    before = jnp.cumsum(onehot, axis=0) - onehot
    target = flat_ids * capacity + jnp.sum(before * onehot, axis=1)
    pair_slot = target.reshape(token_count, top_count)
    picker = jnp.any(
        pair_slot[None, :, :] == jnp.arange(slot_count, dtype=jnp.int32)[:, None, None], axis=2
    ).astype(jnp.bfloat16)
    slot_in = jnp.dot(picker, normed, preferred_element_type=jnp.float32).astype(jnp.bfloat16)
    slot_grad = jnp.dot(picker, grad_rows, preferred_element_type=jnp.float32).astype(jnp.bfloat16)
    wide_shape = (experts, SLICES, capacity, feature_width)
    spread_in = jnp.broadcast_to(
        slot_in.reshape(experts, 1, capacity, feature_width), wide_shape
    ).reshape(devices, capacity, feature_width)
    spread_grad = jnp.broadcast_to(
        slot_grad.reshape(experts, 1, capacity, feature_width), wide_shape
    ).reshape(devices, capacity, feature_width)
    rows_in = lax.all_to_all(spread_in, "expert", split_axis=0, concat_axis=0, tiled=True)
    rows_back = lax.all_to_all(spread_grad, "expert", split_axis=0, concat_axis=0, tiled=True)
    item_count = rows_in.shape[1]
    out_rows, back_rows = run_rows(
        rows_in.reshape(-1, feature_width), rows_back.reshape(-1, feature_width)
    )
    back_out = lax.all_to_all(
        out_rows.reshape(devices, item_count, feature_width),
        "expert",
        split_axis=0,
        concat_axis=0,
        tiled=True,
    )
    back_grad = lax.all_to_all(
        back_rows.reshape(devices, item_count, feature_width),
        "expert",
        split_axis=0,
        concat_axis=0,
        tiled=True,
    )
    merged_out = jnp.sum(back_out.reshape(wide_shape).astype(jnp.float32), axis=1).reshape(
        slot_count, feature_width
    )
    merged_grad = jnp.sum(back_grad.reshape(wide_shape).astype(jnp.float32), axis=1).reshape(
        slot_count, feature_width
    )
    weights = route_weights[:, :, None]
    mixed_rows = jnp.sum(jnp.take(merged_out, pair_slot, axis=0) * weights, axis=1)
    grad_normed = jnp.sum(jnp.take(merged_grad, pair_slot, axis=0) * weights, axis=1)
    layer_out = (values + mixed_rows).astype(jnp.bfloat16)
    scaled = grad_normed * gain_wide
    cubed = inverse * inverse * inverse
    grad_in = (
        grad_rows.astype(jnp.float32)
        + inverse * scaled
        - values * cubed * jnp.mean(scaled * values, axis=-1, keepdims=True)
    ).astype(jnp.bfloat16)
    next_rows = shifted(layer_out, "pipe", 1)
    prev_rows = shifted(grad_in, "pipe", -1)
    return (next_rows[None], prev_rows[None])


def solution(mesh):
    return jax.shard_map(
        body,
        mesh=mesh,
        in_specs=(
            P("pipe", "expert", None),
            P("pipe", "expert", None),
            P("pipe", None),
            P("pipe", "expert", None),
            P("pipe", "expert", None),
            P("pipe", None, "expert"),
            P("pipe", None, "expert"),
            P("pipe", "expert", None),
        ),
        out_specs=(P("pipe", "expert", None), P("pipe", "expert", None)),
        check_vma=False,
    )
```

profile of v0, /device:TPU:18, one launch (start us, length us, event | category | flops | bytes accessed | tf_op | source)
XLA Modules:
  0.0 1826.2 jit_solution(5359203299982551610)
XLA Ops:
  9.7 6.5 broadcast_in_dim.34
  16.3 6.3 all-to-all-start
  26.0 392.6 %all-to-all-done = bf16[16,80,7168]{2,1,0:T(8,128)(2,1)} async-done(((bf16[16,80,7168]{2,1,0:T(8,128)(2,1)}), bf16[16,80,7168]{2,1,0:T(8,128)(2,1)}, u32[]{:S(2)}, u32[]{:S(2)}) %all-to-all-start) | async-done | bytes 18350112 | tf_op jit(solution)/shard_map/all_to_all | solution.py:80
  418.6 8.0 broadcast_in_dim.37
  426.7 5.3 all-to-all-start.2
  432.0 10.0 fusion.18
  442.0 8.8 fusion.14
  450.7 376.9 %all-to-all-done.2 = bf16[16,80,7168]{2,1,0:T(8,128)(2,1)} async-done(((bf16[16,80,7168]{2,1,0:T(8,128)(2,1)}), bf16[16,80,7168]{2,1,0:T(8,128)(2,1)}, u32[]{:S(2)}, u32[]{:S(2)}) %all-to-all-start.2) | async-done | bytes 18350112 | tf_op jit(solution)/shard_map/all_to_all | solution.py:81
  827.6 9.9 fusion.10
  838.5 16.5 fusion.16
  855.1 21.9 %add_convert_fusion = bf16[1280,7168]{1,0:T(8,128)(2,1)} fusion(f32[1280,7168]{1,0:T(8,128)} %fusion.16, bf16[1,7168,256]{2,1,0:T(8,128)(2,1)} %param.16, f32[1280,256]{1,0:T(8,128)} %copy-done.1, f32[1280,256]{1,0:T(8,128)S(1)} %fusion.18), kind=kOutput, calls=%fused_computation.4 | convolution fusion | flops 4717936640 | bytes 61341696 | tf_op jit(solution)/shard_map/dot_general | solution.py:21
  876.9 5.3 all-to-all-start.3
  882.3 10.9 convolution_convert_fusion
  893.2 384.7 %all-to-all-done.3 = bf16[16,80,7168]{2,1,0:T(8,128)(2,1)} async-done(((bf16[16,80,7168]{2,1,0:T(8,128)(2,1)}), bf16[16,80,7168]{2,1,0:T(8,128)(2,1)}, u32[]{:S(2)}, u32[]{:S(2)}) %all-to-all-start.3) | async-done | bytes 18350112 | tf_op jit(solution)/shard_map/all_to_all | solution.py:93
  1283.9 13.6 convert_reduce_fusion
  1297.4 12.4 gather_fusion.1
  1309.9 9.3 reshape.126
  1319.2 359.7 %all-to-all-done.1 = bf16[16,80,7168]{2,1,0:T(8,128)(2,1)} async-done(((bf16[16,80,7168]{2,1,0:T(8,128)(2,1)}), bf16[16,80,7168]{2,1,0:T(8,128)(2,1)}, u32[]{:S(2)}, u32[]{:S(2)}) %all-to-all-start.1) | async-done | bytes 18350112 | tf_op jit(solution)/shard_map/all_to_all | solution.py:86
  1678.8 13.8 convert_reduce_fusion.1
  1692.7 12.4 gather_fusion
  1705.1 9.3 reshape.122
  1714.4 24.3 %fusion = (f32[128,7168]{1,0:T(8,128)S(1)}, f32[128,7168]{1,0:T(8,128)S(1)}) fusion(f32[128,2,7168]{2,1,0:T(2,128)} %reshape.126, pred[128,2]{1,0:T(8,128)(4,1)S(1)} %copy.34, f32[128,2]{1,0:T(8,128)S(1)} %copy.37, f32[128,2,7168]{2,1,0:T(2,128)} %reshape.122), kind=kLoop, calls=%fused_computation.14 | loop fusion | flops 9175040 | bytes 22021376 | tf_op jit(solution)/shard_map/reduce_sum | solution.py:108
  1744.2 40.9 %collective-permute-done = bf16[128,7168]{1,0:T(8,128)(2,1)S(1)} collective-permute-done((bf16[128,7168]{1,0:T(8,128)(2,1)S(1)}, bf16[128,7168]{1,0:T(8,128)(2,1)S(1)}, u32[]{:S(2)}, u32[]{:S(2)}) %collective-permute-start) | collective-permute-done | bytes 1835040 | tf_op jit(solution)/shard_map/ppermute | solution.py:17
  1785.1 38.2 %collective-permute-done.1 = bf16[128,7168]{1,0:T(8,128)(2,1)S(1)} collective-permute-done((bf16[128,7168]{1,0:T(8,128)(2,1)S(1)}, bf16[128,7168]{1,0:T(8,128)(2,1)S(1)}, u32[]{:S(2)}, u32[]{:S(2)}) %collective-permute-start.1) | collective-permute-done | bytes 1835040 | tf_op jit(solution)/shard_map/ppermute | solution.py:17
  (58 shorter events, 27.4 us)
Async XLA Ops:
  6.8 3.0 copy-start.7
  16.3 6.3 copy-start.2
  16.3 402.4 %all-to-all-start = ((bf16[16,80,7168]{2,1,0:T(8,128)(2,1)}), bf16[16,80,7168]{2,1,0:T(8,128)(2,1)}, u32[]{:S(2)}, u32[]{:S(2)}) async-start(bf16[16,80,7168]{2,1,0:T(8,128)(2,1)} %bitcast.85), calls=%async_computation | async-start | bytes 36700160 | tf_op jit(solution)/shard_map/all_to_all | solution.py:80
  426.7 400.9 %all-to-all-start.2 = ((bf16[16,80,7168]{2,1,0:T(8,128)(2,1)}), bf16[16,80,7168]{2,1,0:T(8,128)(2,1)}, u32[]{:S(2)}, u32[]{:S(2)}) async-start(bf16[16,80,7168]{2,1,0:T(8,128)(2,1)} %bitcast.84), calls=%async_computation.2 | async-start | bytes 36700160 | tf_op jit(solution)/shard_map/all_to_all | solution.py:81
  432.0 10.0 copy-start.4
  837.5 1.1 copy-start.1
  876.9 401.0 %all-to-all-start.3 = ((bf16[16,80,7168]{2,1,0:T(8,128)(2,1)}), bf16[16,80,7168]{2,1,0:T(8,128)(2,1)}, u32[]{:S(2)}, u32[]{:S(2)}) async-start(bf16[16,80,7168]{2,1,0:T(8,128)(2,1)} %bitcast.83), calls=%async_computation.3 | async-start | bytes 36700160 | tf_op jit(solution)/shard_map/all_to_all | solution.py:93
  1277.9 5.4 copy-start.6
  1277.9 5.9 copy-start.9
  1277.9 400.9 %all-to-all-start.1 = ((bf16[16,80,7168]{2,1,0:T(8,128)(2,1)}), bf16[16,80,7168]{2,1,0:T(8,128)(2,1)}, u32[]{:S(2)}, u32[]{:S(2)}) async-start(bf16[16,80,7168]{2,1,0:T(8,128)(2,1)} %bitcast.82), calls=%async_computation.1 | async-start | bytes 36700160 | tf_op jit(solution)/shard_map/all_to_all | solution.py:86
  1714.3 24.4 %copy-start = (bf16[1,128,7168]{2,1,0:T(8,128)(2,1)S(1)}, bf16[1,128,7168]{2,1,0:T(8,128)(2,1)}, u32[]{:S(2)}) copy-start(bf16[1,128,7168]{2,1,0:T(8,128)(2,1)} %param.10) | copy-start | bytes 5505028
  1714.3 24.4 %copy-start.5 = (f32[1,7168]{1,0:T(1,128)S(1)}, f32[1,7168]{1,0:T(1,128)}, u32[]{:S(2)}) copy-start(f32[1,7168]{1,0:T(1,128)} %param.12) | copy-start | bytes 86020
  1738.7 1.5 copy-start.3
  1738.7 1.5 copy-start.8
  1738.7 1.5 copy-start.10
  1742.1 43.0 %collective-permute-start = (bf16[128,7168]{1,0:T(8,128)(2,1)S(1)}, bf16[128,7168]{1,0:T(8,128)(2,1)S(1)}, u32[]{:S(2)}, u32[]{:S(2)}) collective-permute-start(bf16[128,7168]{1,0:T(8,128)(2,1)S(1)} %get-tuple-element.8), channel_id=1, source_target_pairs={{0,16},{16,0},{1,17},{17,1},{2,18},{18,2},{3,19},{19,3},{4,20},{20... | collective-permute-start | bytes 5505032 | tf_op jit(solution)/shard_map/ppermute | solution.py:17
  1742.7 80.5 %collective-permute-start.1 = (bf16[128,7168]{1,0:T(8,128)(2,1)S(1)}, bf16[128,7168]{1,0:T(8,128)(2,1)S(1)}, u32[]{:S(2)}, u32[]{:S(2)}) collective-permute-start(bf16[128,7168]{1,0:T(8,128)(2,1)S(1)} %get-tuple-element.7), channel_id=1, source_target_pairs={{0,16},{16,0},{1,17},{17,1},{2,18},{18,2},{3,19},{19,3},{4,20},{20... | collective-permute-start | bytes 5505032 | tf_op jit(solution)/shard_map/ppermute | solution.py:17
where the time goes:
time: 1830 us
  waiting for transfers between devices  1590 us (87%)
  matrix products  84.3 us (5%)
  local copies, waits for them, and re-layouts  64.6 us (4%)
  other arithmetic  58.8 us (3%)
  starting transfers between devices  24.3 us (1%)
    all_to_all x1, waiting for transfers between devices, body(): lax.all_to_all(spread_in, 'expert', split_axis=0, concat_axis=0, tiled=True)  393 us
    all_to_all x1, waiting for transfers between devices, body(): lax.all_to_all(back_rows.reshape(devices, item_count, feature_width), 'ex...  385 us
    all_to_all x1, waiting for transfers between devices, body(): lax.all_to_all(spread_grad, 'expert', split_axis=0, concat_axis=0, tiled=...  377 us
    all_to_all x1, waiting for transfers between devices, body(): lax.all_to_all(out_rows.reshape(devices, item_count, feature_width), 'exp...  360 us
    ppermute x2, waiting for transfers between devices, shifted(): return lax.ppermute(value, axis, pairs)  79 us
    dot_general x3, matrix products, transpose_dot(): lax.dot_general(left_arr, right_arr, (((1,), (1,)), ((), ())), preferred_...  48.3 us
  transfers between devices with their start and end apart: 6, of which 6 were waited for; matrix products, arithmetic and copies ran while one was open for 4% of the time, Pallas kernels for 0%

commit v1 on v0

v1 whole, which is shorter than its diff:
```python
import jax
import jax.numpy as jnp
from jax import lax
from jax.experimental import pallas as pl
from jax.experimental.pallas import tpu as pltpu
from jax.sharding import PartitionSpec as P

SLICES = 4
EPSILON = 1e-06
BF16 = jnp.bfloat16
F32 = jnp.float32


def move(value, pipe_steps, expert_map):
    pipes, devices = lax.axis_size("pipe"), lax.axis_size("expert")
    pairs = [
        (p * devices + d, ((p + pipe_steps) % pipes) * devices + expert_map(d))
        for p in range(pipes)
        for d in range(devices)
    ]
    return lax.ppermute(value, ("pipe", "expert"), pairs)


def dot_nt(left_arr, right_arr):
    return lax.dot_general(
        left_arr, right_arr, (((1,), (1,)), ((), ())), preferred_element_type=F32
    )


def dot_nn(left_arr, right_arr):
    return jnp.dot(left_arr, right_arr, preferred_element_type=F32)


def tile_of(width):
    for tile in (1024, 512, 256, 128):
        if width % tile == 0:
            return tile
    return width


def out_rows(hidden, downs, blocks, first, width):
    rows, ffd = hidden.shape[0], downs[0].shape[0]
    capacity = rows // blocks
    tile = tile_of(width)
    base = first // tile

    def kernel(h_ref, *refs):
        down_refs, out_refs = refs[:SLICES], refs[SLICES:]
        total = dot_nn(h_ref[:, 0:ffd], down_refs[0][...])
        for j in range(1, SLICES):
            total += dot_nn(h_ref[:, j * ffd : (j + 1) * ffd], down_refs[j][...])
        for s in range(blocks):
            out_refs[s][...] = total[s * capacity : (s + 1) * capacity].astype(BF16)

    return pl.pallas_call(
        kernel,
        grid=(width // tile,),
        in_specs=[pl.BlockSpec((rows, SLICES * ffd), lambda i: (0, 0))]
        + [pl.BlockSpec((ffd, tile), lambda i: (0, i + base))] * SLICES,
        out_specs=[pl.BlockSpec((capacity, tile), lambda i: (0, i))] * blocks,
        out_shape=[jax.ShapeDtypeStruct((capacity, width), BF16)] * blocks,
        compiler_params=pltpu.CompilerParams(vmem_limit_bytes=40 * 1024 * 1024),
        cost_estimate=pl.CostEstimate(
            flops=2 * rows * SLICES * ffd * width,
            bytes_accessed=2 * width * (SLICES * ffd + rows),
            transcendentals=0,
        ),
        name="out_rows",
    )(hidden, *downs)


def grad_rows_back(grad_gate, grad_up, gates, ups, blocks, first, width):
    rows, ffd = grad_gate.shape[0], gates[0].shape[1]
    capacity = rows // blocks
    tile = tile_of(width)
    base = first // tile

    def kernel(g_ref, u_ref, *refs):
        gate_refs, up_refs, out_refs = refs[:SLICES], refs[SLICES : 2 * SLICES], refs[2 * SLICES :]
        total = None
        for j in range(SLICES):
            cols = slice(j * ffd, (j + 1) * ffd)
            part = dot_nt(g_ref[:, cols], gate_refs[j][...]) + dot_nt(u_ref[:, cols], up_refs[j][...])
            total = part if total is None else total + part
        for s in range(blocks):
            out_refs[s][...] = total[s * capacity : (s + 1) * capacity].astype(BF16)

    return pl.pallas_call(
        kernel,
        grid=(width // tile,),
        in_specs=[pl.BlockSpec((rows, SLICES * ffd), lambda i: (0, 0))] * 2
        + [pl.BlockSpec((tile, ffd), lambda i: (i + base, 0))] * (2 * SLICES),
        out_specs=[pl.BlockSpec((capacity, tile), lambda i: (0, i))] * blocks,
        out_shape=[jax.ShapeDtypeStruct((capacity, width), BF16)] * blocks,
        compiler_params=pltpu.CompilerParams(vmem_limit_bytes=40 * 1024 * 1024),
        cost_estimate=pl.CostEstimate(
            flops=4 * rows * SLICES * ffd * width,
            bytes_accessed=2 * width * (2 * SLICES * ffd + rows),
            transcendentals=0,
        ),
        name="grad_rows",
    )(grad_gate, grad_up, *gates, *ups)


def slots_of(route_ids, home, experts, capacity):
    token_count, top_count = route_ids.shape
    relative = (route_ids.reshape(-1) - home + experts) % experts
    onehot = (relative[:, None] == jnp.arange(experts, dtype=jnp.int32)[None, :]).astype(jnp.int32)
    before = jnp.cumsum(onehot, axis=0) - onehot
    target = relative * capacity + jnp.sum(before * onehot, axis=1)
    return target.reshape(token_count, top_count)


def gather_slices(weight):
    far = move(weight, 0, lambda d: d ^ 2)
    near = move(weight, 0, lambda d: d ^ 1)
    cross = move(far, 0, lambda d: d ^ 1)
    return [weight, near, far, cross]


def pick_back(pair_slot, weights, back, experts, capacity):
    slots = jnp.arange(experts * capacity, dtype=jnp.int32)[None, :]
    rows = jnp.concatenate(back, axis=0)
    total = None
    for k in range(pair_slot.shape[1]):
        picker = (pair_slot[:, k : k + 1] == slots).astype(BF16)
        part = dot_nn(picker, rows) * weights[:, k : k + 1]
        total = part if total is None else total + part
    return total


def inverse_of(values):
    return lax.rsqrt(jnp.mean(values * values, axis=-1, keepdims=True) + EPSILON)


def body(tokens, grad_out, norm_gain, expert_ids, gate_weights, w_gate, w_up, w_down):
    tokens = tokens[0]
    grad_rows = grad_out[0]
    gain = norm_gain[0][None, :]
    route_ids = expert_ids[0]
    route_weights = gate_weights[0]
    token_count, width = tokens.shape
    top_count = route_ids.shape[1]
    devices = lax.axis_size("expert")
    pipes = lax.axis_size("pipe")
    experts = devices // SLICES
    step_size = 4 * experts * SLICES
    capacity = min(
        token_count, SLICES * ((token_count * top_count * 5 + step_size - 1) // step_size)
    )
    home = lax.axis_index("expert") // SLICES
    same = lambda d: d

    gates, ups, downs = gather_slices(w_gate[0]), gather_slices(w_up[0]), gather_slices(w_down[0])

    routing = jnp.concatenate([route_ids.astype(F32), route_weights], axis=1)
    routing_next = move(routing, 1, same)
    tokens_next = move(tokens, 1, same)
    if pipes == 2:
        routing_prev, tokens_prev = routing_next, tokens_next
    else:
        routing_prev = move(routing, -1, same)
        tokens_prev = move(tokens, -1, same)
    grad_prev = move(grad_rows, -1, same)
    gain_prev = move(gain, -1, same)

    values = tokens.astype(F32)
    normed = (values * inverse_of(values) * gain).astype(BF16)
    pair_slot = slots_of(route_ids, home, experts, capacity)
    pickers = [
        jnp.any(
            pair_slot[None, :, :]
            == (s * capacity + jnp.arange(capacity, dtype=jnp.int32))[:, None, None],
            axis=2,
        ).astype(BF16)
        for s in range(experts)
    ]

    def dispatch(rows):
        blocks = []
        for s in range(experts):
            block = dot_nn(pickers[s], rows).astype(BF16)
            if s:
                block = move(block, 0, lambda d, s=s: (d + SLICES * s) % devices)
            blocks.append(block)
        return jnp.concatenate(blocks, axis=0)

    rows_in = dispatch(normed)
    rows_back = dispatch(grad_rows)

    hidden, gates_grad, ups_grad = [], [], []
    for j in range(SLICES):
        gate_pre = dot_nn(rows_in, gates[j])
        up_pre = dot_nn(rows_in, ups[j])
        sig = jax.nn.sigmoid(gate_pre)
        swish = gate_pre * sig
        hidden.append((swish * up_pre).astype(BF16))
        grad_hidden = dot_nt(rows_back, downs[j])
        gates_grad.append((grad_hidden * up_pre * sig * (1.0 + gate_pre * (1.0 - sig))).astype(BF16))
        ups_grad.append((grad_hidden * swish).astype(BF16))
    hidden = jnp.concatenate(hidden, axis=1)
    gates_grad = jnp.concatenate(gates_grad, axis=1)
    ups_grad = jnp.concatenate(ups_grad, axis=1)

    def send_back(blocks, pipe_steps):
        return [
            move(block, pipe_steps, lambda d, s=s: (d - SLICES * s) % devices)
            for s, block in enumerate(blocks)
        ]

    back_out = send_back(out_rows(hidden, downs, experts, 0, width), 1)
    back_grad = send_back(grad_rows_back(gates_grad, ups_grad, gates, ups, experts, 0, width), -1)

    def routing_of(table):
        ids = table[:, :top_count].astype(jnp.int32)
        return slots_of(ids, home, experts, capacity), table[:, top_count:]

    slot_next, weights_next = routing_of(routing_next)
    slot_prev, weights_prev = routing_of(routing_prev)
    mixed = pick_back(slot_next, weights_next, back_out, experts, capacity)
    next_rows = (tokens_next.astype(F32) + mixed).astype(BF16)

    scaled = pick_back(slot_prev, weights_prev, back_grad, experts, capacity) * gain_prev
    values_prev = tokens_prev.astype(F32)
    inverse = inverse_of(values_prev)
    cubed = inverse * inverse * inverse
    prev_rows = (
        grad_prev.astype(F32)
        + inverse * scaled
        - values_prev * cubed * jnp.mean(scaled * values_prev, axis=-1, keepdims=True)
    ).astype(BF16)
    return (next_rows[None], prev_rows[None])


def solution(mesh):
    return jax.shard_map(
        body,
        mesh=mesh,
        in_specs=(
            P("pipe", "expert", None),
            P("pipe", "expert", None),
            P("pipe", None),
            P("pipe", "expert", None),
            P("pipe", "expert", None),
            P("pipe", None, "expert"),
            P("pipe", None, "expert"),
            P("pipe", "expert", None),
        ),
        out_specs=(P("pipe", "expert", None), P("pipe", "expert", None)),
        check_vma=False,
    )
```

time: 1830 us -> 657 us (0.36)
  waiting for transfers between devices: 1590 us -> 503 us
  local copies, waits for them, and re-layouts: 64.6 us -> 10.9 us
  other arithmetic: 58.8 us -> 20 us
  Pallas kernels: 0 us -> 24.4 us
  matrix products: 84.3 us -> 64.7 us
    all_to_all x4 -> x0, waiting for transfers between devices: 1510 us -> none  [the longest x1 393 us: body(): lax.all_to_all(spread_in, 'expert', split_axis=0, concat_axis=0, tiled=True)]
    ppermute x2 -> x27, waiting for transfers between devices: 79 us -> 503 us  [move(): return lax.ppermute(value, ('pipe', 'expert'), pairs)]
    reduce_sum x6 -> x3, other arithmetic: 54.2 us -> 1.98 us  [the longest x1 1.93 us: inverse_of(): jnp.mean(values * values, axis=-1, keepdims=True) + EPSILON]
    gather x4 -> x0, local copies, waits for them, and re-layouts: 43.4 us -> none  [the longest x2 21.7 us: body(): jnp.take(merged_grad, pair_slot, axis=0) * weights]
    ppermute x2 -> x27, starting transfers between devices: 2.09 us -> 30.1 us  [move(): return lax.ppermute(value, ('pipe', 'expert'), pairs)]
    pallas_call x0 -> x2, Pallas kernels: none -> 24.4 us  [the longest x1 15.6 us: grad_rows_back(): pl.pallas_call(kernel, grid=(width // tile,), in_specs=[pl.BlockSpec((row...]
    all_to_all x4 -> x0, starting transfers between devices: 22.2 us -> none  [the longest x1 6.32 us: body(): lax.all_to_all(spread_in, 'expert', split_axis=0, concat_axis=0, tiled=True)]
    dot_general x8 -> x24, matrix products: 84.3 us -> 64.7 us  [the longest x20 56.1 us: dot_nn(): return jnp.dot(left_arr, right_arr, preferred_element_type=F32)]
  transfers between devices with their start and end apart: 6 -> 27, of which waited for: 6 -> 14; matrix products, arithmetic and copies ran while one was open for 4% -> 13% of each run, Pallas kernels for 0% -> 4%
where the time goes in v1:
time: 657 us; the launch traced here: 654 us
  waiting for transfers between devices  503 us (77%)
  matrix products  64.7 us (10%)
  starting transfers between devices  30.1 us (5%)
  Pallas kernels  24.4 us (4%)
  other arithmetic  20 us (3%)
  local copies, waits for them, and re-layouts  10.9 us (2%)
    ppermute x27, waiting for transfers between devices, move(): return lax.ppermute(value, ('pipe', 'expert'), pairs)  503 us
    dot_general x20, matrix products, dot_nn(): return jnp.dot(left_arr, right_arr, preferred_element_type=F32)  56.1 us
    ppermute x27, starting transfers between devices, move(): return lax.ppermute(value, ('pipe', 'expert'), pairs)  30.1 us
    pallas_call x1, Pallas kernels, grad_rows_back(): pl.pallas_call(kernel, grid=(width // tile,), in_specs=[pl.BlockSpec((row...  15.6 us
  transfers between devices with their start and end apart: 27, of which 14 were waited for; matrix products, arithmetic and copies ran while one was open for 13% of the time, Pallas kernels for 4%

profile of v1, /device:TPU:18, one launch (start us, length us, event | category | flops | bytes accessed | tf_op | source)
XLA Modules:
  0.0 654.4 jit_solution(4639983252060606584)
XLA Ops:
  15.8 3.9 collective-permute-start.3
  36.0 3.5 collective-permute-start.2
  42.5 18.1 %collective-permute-done.4 = bf16[80,7168]{1,0:T(8,128)(2,1)S(1)} collective-permute-done((bf16[80,7168]{1,0:T(8,128)(2,1)S(1)}, bf16[80,7168]{1,0:T(8,128)(2,1)S(1)}, u32[]{:S(2)}, u32[]{:S(2)}) %collective-permute-start.4) | collective-permute-done | bytes 1146912 | tf_op jit(solution)/shard_map/ppermute | solution.py:21
  64.7 92.2 %collective-permute-done.3 = bf16[80,7168]{1,0:T(8,128)(2,1)} collective-permute-done((bf16[80,7168]{1,0:T(8,128)(2,1)}, bf16[80,7168]{1,0:T(8,128)(2,1)}, u32[]{:S(2)}, u32[]{:S(2)}) %collective-permute-start.3) | collective-permute-done | bytes 1146912 | tf_op jit(solution)/shard_map/ppermute | solution.py:21
  158.6 21.5 %collective-permute-done.20 = bf16[80,7168]{1,0:T(8,128)(2,1)} collective-permute-done((bf16[80,7168]{1,0:T(8,128)(2,1)}, bf16[80,7168]{1,0:T(8,128)(2,1)}, u32[]{:S(2)}, u32[]{:S(2)}) %collective-permute-start.20) | collective-permute-done | bytes 1146912 | tf_op jit(solution)/shard_map/ppermute | solution.py:21
  180.1 4.1 collective-permute-done.2
  189.4 19.2 %collective-permute-done.19 = bf16[80,7168]{1,0:T(8,128)(2,1)S(1)} collective-permute-done((bf16[80,7168]{1,0:T(8,128)(2,1)}, bf16[80,7168]{1,0:T(8,128)(2,1)S(1)}, u32[]{:S(2)}, u32[]{:S(2)}) %collective-permute-start.19) | collective-permute-done | bytes 1146912 | tf_op jit(solution)/shard_map/ppermute | solution.py:21
  208.6 4.8 pad_maximum_fusion.1
  214.0 3.4 fusion.51
  219.6 19.9 %collective-permute-done.8.refs_6_ = bf16[7168,256]{1,0:T(8,128)(2,1)S(1)} collective-permute-done((bf16[7168,256]{1,0:T(8,128)(2,1)}, bf16[7168,256]{1,0:T(8,128)(2,1)S(1)}, u32[]{:S(2)}, u32[]{:S(2)}) %collective-permute-start.8) | collective-permute-done | bytes 3670048 | tf_op jit(solution)/shard_map/ppermute | solution.py:21
  239.5 4.7 fusion.59
  244.2 70.1 %collective-permute-done.12.refs_2_ = bf16[256,7168]{1,0:T(8,128)(2,1)S(1)} collective-permute-done((bf16[256,7168]{1,0:T(8,128)(2,1)}, bf16[256,7168]{1,0:T(8,128)(2,1)S(1)}, u32[]{:S(2)}, u32[]{:S(2)}) %collective-permute-start.12) | collective-permute-done | bytes 3670048 | tf_op jit(solution)/shard_map/ppermute | solution.py:21
  315.7 3.4 fusion.57
  339.7 15.6 %grad_rows.1 = (bf16[80,7168]{1,0:T(8,128)(2,1)}, bf16[80,7168]{1,0:T(8,128)(2,1)S(1)}, bf16[80,7168]{1,0:T(8,128)(2,1)S(1)}, bf16[80,7168]{1,0:T(8,128)(2,1)S(1)}) custom-call(bf16[320,1024]{1,0:T(8,128)(2,1)S(1)} %pad_maximum_fusion.3.g_ref, bf16[320,1024]{1,0:T(8,128)(2,1)S(1)} %pad_maximum_fusion.4.u_ref, bf16[7168,256]{1,0:T(8,128)(2,1)} %bitcast.9.refs_0_, ...), custom_call_target="tpu_custom_call" | custom-call | flops 9395240960 | bytes 33947648 | tf_op jit(solution)/shard_map/grad_rows/pallas_call | solution.py:88
  362.0 8.7 %out_rows.1 = (bf16[80,7168]{1,0:T(8,128)(2,1)S(1)}, bf16[80,7168]{1,0:T(8,128)(2,1)S(1)}, bf16[80,7168]{1,0:T(8,128)(2,1)S(1)}, bf16[80,7168]{1,0:T(8,128)(2,1)S(1)}) custom-call(bf16[320,1024]{1,0:T(8,128)(2,1)S(1)} %pad_maximum_fusion.2.h_ref, bf16[256,7168]{1,0:T(8,128)(2,1)S(1)} %bitcast.111, bf16[256,7168]{1,0:T(8,128)(2,1)S(1)} %copy-done.3, ...), custom_call_target="tpu_custom_call" | custom-call | flops 4697620480 | bytes 19267584 | tf_op jit(solution)/shard_map/out_rows/pallas_call | solution.py:55
  372.7 60.6 %collective-permute-done.22 = bf16[80,7168]{1,0:T(8,128)(2,1)} collective-permute-done((bf16[80,7168]{1,0:T(8,128)(2,1)}, bf16[80,7168]{1,0:T(8,128)(2,1)}, u32[]{:S(2)}, u32[]{:S(2)}) %collective-permute-start.22) | collective-permute-done | bytes 1146912 | tf_op jit(solution)/shard_map/ppermute | solution.py:21
  434.6 47.0 %collective-permute-done.14 = bf16[80,7168]{1,0:T(8,128)(2,1)S(1)} collective-permute-done((bf16[80,7168]{1,0:T(8,128)(2,1)S(1)}, bf16[80,7168]{1,0:T(8,128)(2,1)S(1)}, u32[]{:S(2)}, u32[]{:S(2)}) %collective-permute-start.14) | collective-permute-done | bytes 1146912 | tf_op jit(solution)/shard_map/ppermute | solution.py:21
  485.2 55.8 %collective-permute-done.24 = bf16[80,7168]{1,0:T(8,128)(2,1)S(1)} collective-permute-done((bf16[80,7168]{1,0:T(8,128)(2,1)S(1)}, bf16[80,7168]{1,0:T(8,128)(2,1)S(1)}, u32[]{:S(2)}, u32[]{:S(2)}) %collective-permute-start.24) | collective-permute-done | bytes 1146912 | tf_op jit(solution)/shard_map/ppermute | solution.py:21
  541.1 4.3 collective-permute-start.16
  553.0 17.1 %collective-permute-done.15 = bf16[80,7168]{1,0:T(8,128)(2,1)S(1)} collective-permute-done((bf16[80,7168]{1,0:T(8,128)(2,1)S(1)}, bf16[80,7168]{1,0:T(8,128)(2,1)S(1)}, u32[]{:S(2)}, u32[]{:S(2)}) %collective-permute-start.15) | collective-permute-done | bytes 1146912 | tf_op jit(solution)/shard_map/ppermute | solution.py:21
  570.1 69.6 %collective-permute-done.16 = bf16[80,7168]{1,0:T(8,128)(2,1)S(1)} collective-permute-done((bf16[80,7168]{1,0:T(8,128)(2,1)S(1)}, bf16[80,7168]{1,0:T(8,128)(2,1)S(1)}, u32[]{:S(2)}, u32[]{:S(2)}) %collective-permute-start.16) | collective-permute-done | bytes 1146912 | tf_op jit(solution)/shard_map/ppermute | solution.py:21
  639.8 4.7 collective-permute-done.17
  645.8 4.0 fusion.5
  649.8 4.6 fusion.14
  (133 shorter events, 92.4 us)
Async XLA Ops:
  2.8 29.8 %collective-permute-start.1 = (f32[128,4]{1,0:T(8,128)}, f32[128,4]{1,0:T(8,128)S(1)}, u32[]{:S(2)}, u32[]{:S(2)}) collective-permute-start(f32[128,4]{1,0:T(8,128)} %copy.46), channel_id=1, source_target_pairs={{0,16},{1,17},{2,18},{3,19},{4,20},{5,21},{6,22},{7,23},{8,24},{9,... | collective-permute-start | bytes 6152 | tf_op jit(solution)/shard_map/ppermute | solution.py:21
  12.5 48.1 %collective-permute-start.4 = (bf16[80,7168]{1,0:T(8,128)(2,1)S(1)}, bf16[80,7168]{1,0:T(8,128)(2,1)S(1)}, u32[]{:S(2)}, u32[]{:S(2)}) collective-permute-start(bf16[80,7168]{1,0:T(8,128)(2,1)S(1)} %convolution_convert_fusion.4), channel_id=1, source_target_pairs={{0,12},{1,13},{2,14},{3,15},{4,0},{5,1},{6,2},{7,3},{8,4},{9,5},{1... | collective-permute-start | bytes 3440648 | tf_op jit(solution)/shard_map/ppermute | solution.py:21
  15.8 141.2 %collective-permute-start.3 = (bf16[80,7168]{1,0:T(8,128)(2,1)}, bf16[80,7168]{1,0:T(8,128)(2,1)}, u32[]{:S(2)}, u32[]{:S(2)}) collective-permute-start(bf16[80,7168]{1,0:T(8,128)(2,1)} %convolution_convert_fusion.5), channel_id=1, source_target_pairs={{0,8},{1,9},{2,10},{3,11},{4,12},{5,13},{6,14},{7,15},{8,0},{9,1},... | collective-permute-start | bytes 3440648 | tf_op jit(solution)/shard_map/ppermute | solution.py:21
  19.7 193.7 %collective-permute-start.7 = (bf16[7168,256]{1,0:T(8,128)(2,1)}, bf16[7168,256]{1,0:T(8,128)(2,1)}, u32[]{:S(2)}, u32[]{:S(2)}) collective-permute-start(bf16[7168,256]{1,0:T(8,128)(2,1)} %bitcast.9.refs_0_), channel_id=1, source_target_pairs={{0,2},{1,3},{2,0},{3,1},{4,6},{5,7},{6,4},{7,5},{8,10},{9,11},{10,... | collective-permute-start | bytes 11010056 | tf_op jit(solution)/shard_map/ppermute | solution.py:21
  32.6 147.4 %collective-permute-start.20 = (bf16[80,7168]{1,0:T(8,128)(2,1)}, bf16[80,7168]{1,0:T(8,128)(2,1)}, u32[]{:S(2)}, u32[]{:S(2)}) collective-permute-start(bf16[80,7168]{1,0:T(8,128)(2,1)} %convolution_convert_fusion.1), channel_id=1, source_target_pairs={{0,8},{1,9},{2,10},{3,11},{4,12},{5,13},{6,14},{7,15},{8,0},{9,1},... | collective-permute-start | bytes 3440648 | tf_op jit(solution)/shard_map/ppermute | solution.py:21
  36.0 148.2 %collective-permute-start.2 = (bf16[80,7168]{1,0:T(8,128)(2,1)}, bf16[80,7168]{1,0:T(8,128)(2,1)}, u32[]{:S(2)}, u32[]{:S(2)}) collective-permute-start(bf16[80,7168]{1,0:T(8,128)(2,1)} %convolution_convert_fusion.6), channel_id=1, source_target_pairs={{0,4},{1,5},{2,6},{3,7},{4,8},{5,9},{6,10},{7,11},{8,12},{9,13},{1... | collective-permute-start | bytes 3440648 | tf_op jit(solution)/shard_map/ppermute | solution.py:21
  60.6 156.8 %collective-permute-start.5 = (bf16[7168,256]{1,0:T(8,128)(2,1)}, bf16[7168,256]{1,0:T(8,128)(2,1)}, u32[]{:S(2)}, u32[]{:S(2)}) collective-permute-start(bf16[7168,256]{1,0:T(8,128)(2,1)} %bitcast.9.refs_0_), channel_id=1, source_target_pairs={{0,1},{1,0},{2,3},{3,2},{4,5},{5,4},{6,7},{7,6},{8,9},{9,8},{10,11... | collective-permute-start | bytes 11010056 | tf_op jit(solution)/shard_map/ppermute | solution.py:21
  157.0 82.5 %collective-permute-start.8 = (bf16[7168,256]{1,0:T(8,128)(2,1)}, bf16[7168,256]{1,0:T(8,128)(2,1)S(1)}, u32[]{:S(2)}, u32[]{:S(2)}) collective-permute-start(bf16[7168,256]{1,0:T(8,128)(2,1)} %bitcast.116), channel_id=1, source_target_pairs={{0,2},{1,3},{2,0},{3,1},{4,6},{5,7},{6,4},{7,5},{8,10},{9,11},{10,... | collective-permute-start | bytes 11010056 | tf_op jit(solution)/shard_map/ppermute | solution.py:21
  184.2 130.1 %collective-permute-start.12 = (bf16[256,7168]{1,0:T(8,128)(2,1)}, bf16[256,7168]{1,0:T(8,128)(2,1)S(1)}, u32[]{:S(2)}, u32[]{:S(2)}) collective-permute-start(bf16[256,7168]{1,0:T(8,128)(2,1)} %bitcast.109), channel_id=1, source_target_pairs={{0,2},{1,3},{2,0},{3,1},{4,6},{5,7},{6,4},{7,5},{8,10},{9,11},{10,... | collective-permute-start | bytes 11010056 | tf_op jit(solution)/shard_map/ppermute | solution.py:21
  208.5 110.6 %collective-permute-start.6 = (bf16[7168,256]{1,0:T(8,128)(2,1)S(1)}, bf16[7168,256]{1,0:T(8,128)(2,1)}, u32[]{:S(2)}, u32[]{:S(2)}) collective-permute-start(bf16[7168,256]{1,0:T(8,128)(2,1)S(1)} %bitcast.118), channel_id=1, source_target_pairs={{0,1},{1,0},{2,3},{3,2},{4,5},{5,4},{6,7},{7,6},{8,9},{9,8},{10,11... | collective-permute-start | bytes 11010056 | tf_op jit(solution)/shard_map/ppermute | solution.py:21
  213.4 112.8 %collective-permute-start.11 = (bf16[256,7168]{1,0:T(8,128)(2,1)S(1)}, bf16[256,7168]{1,0:T(8,128)(2,1)S(1)}, u32[]{:S(2)}, u32[]{:S(2)}) collective-permute-start(bf16[256,7168]{1,0:T(8,128)(2,1)S(1)} %bitcast.110), channel_id=1, source_target_pairs={{0,1},{1,0},{2,3},{3,2},{4,5},{5,4},{6,7},{7,6},{8,9},{9,8},{10,11... | collective-permute-start | bytes 11010056 | tf_op jit(solution)/shard_map/ppermute | solution.py:21
  217.4 111.5 %collective-permute-start.9 = (bf16[7168,256]{1,0:T(8,128)(2,1)}, bf16[7168,256]{1,0:T(8,128)(2,1)}, u32[]{:S(2)}, u32[]{:S(2)}) collective-permute-start(bf16[7168,256]{1,0:T(8,128)(2,1)} %collective-permute-done.7.refs_2_), channel_id=1, source_target_pairs={{0,1},{1,0},{2,3},{3,2},{4,5},{5,4},{6,7},{7,6},{8,9},{9,8},{10,11... | collective-permute-start | bytes 11010056 | tf_op jit(solution)/shard_map/ppermute | solution.py:21
  239.5 94.3 %collective-permute-start.10 = (bf16[7168,256]{1,0:T(8,128)(2,1)S(1)}, bf16[7168,256]{1,0:T(8,128)(2,1)}, u32[]{:S(2)}, u32[]{:S(2)}) collective-permute-start(bf16[7168,256]{1,0:T(8,128)(2,1)S(1)} %collective-permute-done.8.refs_6_), channel_id=1, source_target_pairs={{0,1},{1,0},{2,3},{3,2},{4,5},{5,4},{6,7},{7,6},{8,9},{9,8},{10,11... | collective-permute-start | bytes 11010056 | tf_op jit(solution)/shard_map/ppermute | solution.py:21
  319.1 227.6 %collective-permute-start.26 = (f32[1,7168]{1,0:T(1,128)}, f32[1,7168]{1,0:T(1,128)S(1)}, u32[]{:S(2)}, u32[]{:S(2)}) collective-permute-start(f32[1,7168]{1,0:T(1,128)} %param.10), channel_id=1, source_target_pairs={{0,16},{1,17},{2,18},{3,19},{4,20},{5,21},{6,22},{7,23},{8,24},{9,... | collective-permute-start | bytes 86024 | tf_op jit(solution)/shard_map/ppermute | solution.py:21
  326.2 223.5 %collective-permute-start = (bf16[128,7168]{1,0:T(8,128)(2,1)}, bf16[128,7168]{1,0:T(8,128)(2,1)}, u32[]{:S(2)}, u32[]{:S(2)}) collective-permute-start(bf16[128,7168]{1,0:T(8,128)(2,1)} %bitcast), channel_id=1, source_target_pairs={{0,16},{1,17},{2,18},{3,19},{4,20},{5,21},{6,22},{7,23},{8,24},{9,... | collective-permute-start | bytes 5505032 | tf_op jit(solution)/shard_map/ppermute | solution.py:21
  328.8 321.0 %collective-permute-start.18 = (bf16[128,7168]{1,0:T(8,128)(2,1)}, bf16[128,7168]{1,0:T(8,128)(2,1)}, u32[]{:S(2)}, u32[]{:S(2)}) collective-permute-start(bf16[128,7168]{1,0:T(8,128)(2,1)} %bitcast.13), channel_id=1, source_target_pairs={{0,16},{1,17},{2,18},{3,19},{4,20},{5,21},{6,22},{7,23},{8,24},{9,... | collective-permute-start | bytes 5505032 | tf_op jit(solution)/shard_map/ppermute | solution.py:21
  355.3 77.9 %collective-permute-start.22 = (bf16[80,7168]{1,0:T(8,128)(2,1)}, bf16[80,7168]{1,0:T(8,128)(2,1)}, u32[]{:S(2)}, u32[]{:S(2)}) collective-permute-start(bf16[80,7168]{1,0:T(8,128)(2,1)} %get-tuple-element.14), channel_id=1, source_target_pairs={{0,16},{1,17},{2,18},{3,19},{4,20},{5,21},{6,22},{7,23},{8,24},{9,... | collective-permute-start | bytes 3440648 | tf_op jit(solution)/shard_map/ppermute | solution.py:21
  370.7 110.9 %collective-permute-start.14 = (bf16[80,7168]{1,0:T(8,128)(2,1)S(1)}, bf16[80,7168]{1,0:T(8,128)(2,1)S(1)}, u32[]{:S(2)}, u32[]{:S(2)}) collective-permute-start(bf16[80,7168]{1,0:T(8,128)(2,1)S(1)} %get-tuple-element.10), channel_id=1, source_target_pairs={{0,16},{1,17},{2,18},{3,19},{4,20},{5,21},{6,22},{7,23},{8,24},{9,... | collective-permute-start | bytes 3440648 | tf_op jit(solution)/shard_map/ppermute | solution.py:21
  433.3 51.8 %collective-permute-start.23 = (bf16[80,7168]{1,0:T(8,128)(2,1)S(1)}, bf16[80,7168]{1,0:T(8,128)(2,1)S(1)}, u32[]{:S(2)}, u32[]{:S(2)}) collective-permute-start(bf16[80,7168]{1,0:T(8,128)(2,1)S(1)} %get-tuple-element.15), channel_id=1, source_target_pairs={{0,28},{1,29},{2,30},{3,31},{4,16},{5,17},{6,18},{7,19},{8,20},{9,... | collective-permute-start | bytes 3440648 | tf_op jit(solution)/shard_map/ppermute | solution.py:21
  481.6 59.4 %collective-permute-start.24 = (bf16[80,7168]{1,0:T(8,128)(2,1)S(1)}, bf16[80,7168]{1,0:T(8,128)(2,1)S(1)}, u32[]{:S(2)}, u32[]{:S(2)}) collective-permute-start(bf16[80,7168]{1,0:T(8,128)(2,1)S(1)} %get-tuple-element.16), channel_id=1, source_target_pairs={{0,24},{1,25},{2,26},{3,27},{4,28},{5,29},{6,30},{7,31},{8,16},{9,... | collective-permute-start | bytes 3440648 | tf_op jit(solution)/shard_map/ppermute | solution.py:21
  485.1 56.0 %collective-permute-start.25 = (bf16[80,7168]{1,0:T(8,128)(2,1)S(1)}, bf16[80,7168]{1,0:T(8,128)(2,1)S(1)}, u32[]{:S(2)}, u32[]{:S(2)}) collective-permute-start(bf16[80,7168]{1,0:T(8,128)(2,1)S(1)} %get-tuple-element.17), channel_id=1, source_target_pairs={{0,20},{1,21},{2,22},{3,23},{4,24},{5,25},{6,26},{7,27},{8,28},{9,... | collective-permute-start | bytes 3440648 | tf_op jit(solution)/shard_map/ppermute | solution.py:21
  541.0 29.0 %collective-permute-start.15 = (bf16[80,7168]{1,0:T(8,128)(2,1)S(1)}, bf16[80,7168]{1,0:T(8,128)(2,1)S(1)}, u32[]{:S(2)}, u32[]{:S(2)}) collective-permute-start(bf16[80,7168]{1,0:T(8,128)(2,1)S(1)} %get-tuple-element.11), channel_id=1, source_target_pairs={{0,28},{1,29},{2,30},{3,31},{4,16},{5,17},{6,18},{7,19},{8,20},{9,... | collective-permute-start | bytes 3440648 | tf_op jit(solution)/shard_map/ppermute | solution.py:21
  541.1 98.6 %collective-permute-start.16 = (bf16[80,7168]{1,0:T(8,128)(2,1)S(1)}, bf16[80,7168]{1,0:T(8,128)(2,1)S(1)}, u32[]{:S(2)}, u32[]{:S(2)}) collective-permute-start(bf16[80,7168]{1,0:T(8,128)(2,1)S(1)} %get-tuple-element.12), channel_id=1, source_target_pairs={{0,24},{1,25},{2,26},{3,27},{4,28},{5,29},{6,30},{7,31},{8,16},{9,... | collective-permute-start | bytes 3440648 | tf_op jit(solution)/shard_map/ppermute | solution.py:21
  546.7 97.8 %collective-permute-start.17 = (bf16[80,7168]{1,0:T(8,128)(2,1)S(1)}, bf16[80,7168]{1,0:T(8,128)(2,1)S(1)}, u32[]{:S(2)}, u32[]{:S(2)}) collective-permute-start(bf16[80,7168]{1,0:T(8,128)(2,1)S(1)} %get-tuple-element.13), channel_id=1, source_target_pairs={{0,20},{1,21},{2,22},{3,23},{4,24},{5,25},{6,26},{7,27},{8,28},{9,... | collective-permute-start | bytes 3440648 | tf_op jit(solution)/shard_map/ppermute | solution.py:21
  (12 other events, 211.4 us)

commit v2 on v1

v2 whole, which is shorter than its diff:
```python
import jax
import jax.numpy as jnp
from jax import lax
from jax.experimental import pallas as pl
from jax.experimental.pallas import tpu as pltpu
from jax.sharding import PartitionSpec as P

SLICES = 4
EPSILON = 1e-06
BF16 = jnp.bfloat16
F32 = jnp.float32


def move(value, pipe_steps, expert_map):
    pipes, devices = lax.axis_size("pipe"), lax.axis_size("expert")
    pairs = [
        (p * devices + d, ((p + pipe_steps) % pipes) * devices + expert_map(d))
        for p in range(pipes)
        for d in range(devices)
    ]
    return lax.ppermute(value, ("pipe", "expert"), pairs)


def dot_nt(left_arr, right_arr):
    return lax.dot_general(
        left_arr, right_arr, (((1,), (1,)), ((), ())), preferred_element_type=F32
    )


def dot_nn(left_arr, right_arr):
    return jnp.dot(left_arr, right_arr, preferred_element_type=F32)


def tile_of(width):
    for tile in (1024, 512, 256, 128):
        if width % tile == 0:
            return tile
    return width


MESH = pl.DeviceIdType.MESH
ANY = pl.BlockSpec(memory_space=pl.ANY)


def sections():
    pipe, pipes = lax.axis_index("pipe"), lax.axis_size("pipe")
    return pipe, lax.rem(pipe + 1, pipes), lax.rem(pipe + pipes - 1, pipes)


def greet(partners):
    barrier = pltpu.get_barrier_semaphore()
    for partner in partners:
        pl.semaphore_signal(barrier, inc=1, device_id=partner, device_id_type=MESH)
    pl.semaphore_wait(barrier, len(partners))


def gather_all(slots_in, slots_grad, gate, up, down, tokens, grad_rows):
    experts = slots_in.shape[0]
    devices, pipes = lax.axis_size("expert"), lax.axis_size("pipe")
    two = pipes == 2

    def kernel(si, sg, wg, wu, wd, tok, grd, ri, rg, ag, au, ad, tn, tp, gp, send, recv, local):
        pipe, after, ahead = sections()
        me = lax.axis_index("expert")
        place = lax.rem(me, SLICES)
        base = me - place
        far = base + lax.rem(place + 2, SLICES)
        near = me + 1 - 2 * lax.rem(me, 2)
        others = [(pipe, lax.rem(me + SLICES * s, devices)) for s in range(1, experts)]
        greet(others + [(pipe, far), (pipe, near), (after, me), (ahead, me)])
        count = [0]

        def push(source, target, device):
            n = count[0]
            count[0] += 1
            copy = pltpu.make_async_remote_copy(
                src_ref=source,
                dst_ref=target,
                send_sem=send.at[n],
                recv_sem=recv.at[n],
                device_id=device,
                device_id_type=MESH,
            )
            copy.start()
            return copy

        pairs = [(wg, ag), (wu, au), (wd, ad)]
        fars = [push(w, all_w.at[1], (pipe, far)) for w, all_w in pairs]
        copies = []
        for source, target in ((si, ri), (sg, rg)):
            for s in range(experts - 1, 0, -1):
                copies.append(push(source.at[s], target.at[s], others[s - 1]))
        own = [
            pltpu.make_async_copy(source.at[0], target.at[0], local.at[n])
            for n, (source, target) in enumerate(((si, ri), (sg, rg)))
        ]
        for copy in own:
            copy.start()
        copies += [push(w, all_w.at[0], (pipe, near)) for w, all_w in pairs]
        copies.append(push(tok, tn, (after, me)))
        if not two:
            copies.append(push(tok, tp, (ahead, me)))
        copies.append(push(grd, gp, (ahead, me)))
        for first, (w, all_w) in zip(fars, pairs):
            first.wait()
            copies.append(push(all_w.at[1], all_w.at[2], (pipe, near)))
        for copy in own + copies:
            copy.wait()

    like = lambda value: jax.ShapeDtypeStruct(value.shape, value.dtype)
    three = lambda value: jax.ShapeDtypeStruct((3,) + value.shape, value.dtype)
    total = 2 * (experts - 1) + 9 + (2 if two else 3)
    inputs = (slots_in, slots_grad, gate, up, down, tokens, grad_rows)
    small = jax.ShapeDtypeStruct((16, 128), tokens.dtype)
    outs = pl.pallas_call(
        kernel,
        in_specs=[ANY] * 7,
        out_specs=[ANY] * 8,
        out_shape=[like(slots_in), like(slots_grad), three(gate), three(up), three(down)]
        + [like(tokens), small if two else like(tokens), like(grad_rows)],
        scratch_shapes=[
            pltpu.SemaphoreType.DMA((total,)),
            pltpu.SemaphoreType.DMA((total,)),
            pltpu.SemaphoreType.DMA((2,)),
        ],
        compiler_params=pltpu.CompilerParams(
            collective_id=0, has_side_effects=True, vmem_limit_bytes=VMEM
        ),
        name="gather_all",
    )(*inputs)
    outs = list(outs)
    if two:
        outs[6] = outs[5]
    return outs


VMEM = 58 * 1024 * 1024


def results(hidden, gates_grad, ups_grad, gate, up, down, all_gate, all_up, all_down,
            tok_next, tok_prev, grad_prev, gain_prev, inverse_prev,
            pick_next, wt_next, pick_prev, wt_prev):
    rows, ffd = hidden.shape[0], down.shape[0]
    width = down.shape[1]
    experts, _, capacity = pick_next.shape
    token_count, top = wt_next.shape
    devices = lax.axis_size("expert")
    tile = tile_of(width)
    tiles = width // tile

    def kernel(h, gg, ug, wg, wu, wd, ag, au, ad, tn, tp, gp, gain, inv, pn, wn, pp, wp,
               next_ref, prev_ref, stage_o, stage_g, recv_o, recv_g, scaled, send, recv):
        step = pl.program_id(0)
        pipe, after, ahead = sections()
        me = lax.axis_index("expert")
        homes = [lax.rem(me + devices - SLICES * s, devices) for s in range(experts)]

        @pl.when(step == 0)
        def _():
            greet([(p, d) for p in (after, ahead) for d in homes])

        def cols_of(i):
            return pl.ds(pl.multiple_of(i * tile, tile), tile)

        def copy_of(which, i, s):
            stage, target = ((stage_o, recv_o), (stage_g, recv_g))[which]
            return pltpu.make_async_remote_copy(
                src_ref=stage.at[s, :, cols_of(i)],
                dst_ref=target.at[s, :, cols_of(i)],
                send_sem=send.at[which, i, s],
                recv_sem=recv.at[which, i, s],
                device_id=((after, ahead)[which], homes[s]),
                device_id_type=MESH,
            )

        def ship(which, total):
            stage = (stage_o, stage_g)[which]
            for s in range(experts):
                stage[s, :, cols_of(step)] = total[s * capacity : (s + 1) * capacity].astype(BF16)
            for s in range(experts):
                copy_of(which, step, s).start()

        total = dot_nn(h[:, 0:ffd], wd[...])
        for j in range(1, SLICES):
            total += dot_nn(h[:, j * ffd : (j + 1) * ffd], ad[j - 1])
        ship(0, total)
        total = dot_nt(gg[:, 0:ffd], wg[...]) + dot_nt(ug[:, 0:ffd], wu[...])
        for j in range(1, SLICES):
            part = slice(j * ffd, (j + 1) * ffd)
            total += dot_nt(gg[:, part], ag[j - 1]) + dot_nt(ug[:, part], au[j - 1])
        ship(1, total)

        @pl.when(step == tiles - 1)
        def _():
            def picked(target, pick, weights, cols):
                total = dot_nn(pick[0], target[0, :, cols])
                for s in range(1, experts):
                    total += dot_nn(pick[s], target[s, :, cols])
                value = total[:token_count] * weights[:, 0:1]
                for k in range(1, top):
                    value += total[k * token_count : (k + 1) * token_count] * weights[:, k : k + 1]
                return value

            def finish(i, mean):
                cols = cols_of(i)
                for s in range(experts):
                    copy_of(0, i, s).wait()
                mixed = picked(recv_o, pn, wn, cols)
                next_ref[:, cols] = (tn[:, cols].astype(F32) + mixed).astype(BF16)
                for s in range(experts):
                    copy_of(1, i, s).wait()
                part = picked(recv_g, pp, wp, cols) * gain[:, cols]
                scaled[:, cols] = part
                return mean + jnp.sum(part * tp[:, cols].astype(F32), axis=1, keepdims=True)

            mean = lax.fori_loop(0, tiles, finish, jnp.zeros((token_count, 1), F32)) / width
            inverse = inv[...]
            factor = inverse * inverse * inverse * mean

            def last(i, carry):
                cols = cols_of(i)
                prev_ref[:, cols] = (
                    gp[:, cols].astype(F32)
                    + inverse * scaled[:, cols]
                    - tp[:, cols].astype(F32) * factor
                ).astype(BF16)
                return carry

            lax.fori_loop(0, tiles, last, 0)

    def whole(value):
        return pl.BlockSpec(
            value.shape, lambda i, n=value.ndim: (0,) * n, pipeline_mode=pl.Buffered(1)
        )

    fixed = [tok_next, tok_prev, grad_prev, gain_prev, inverse_prev, pick_next, wt_next, pick_prev, wt_prev]
    in_specs = [whole(hidden), whole(gates_grad), whole(ups_grad)]
    in_specs += [pl.BlockSpec((tile, ffd), lambda i: (i, 0))] * 2
    in_specs += [pl.BlockSpec((ffd, tile), lambda i: (0, i))]
    in_specs += [pl.BlockSpec((3, tile, ffd), lambda i: (0, i, 0))] * 2
    in_specs += [pl.BlockSpec((3, ffd, tile), lambda i: (0, 0, i))]
    in_specs += [whole(value) for value in fixed]
    result = jax.ShapeDtypeStruct((token_count, width), BF16)
    rows_shape = (experts, capacity, width)
    return pl.pallas_call(
        kernel,
        grid=(tiles,),
        in_specs=in_specs,
        out_specs=[pl.BlockSpec((token_count, width), lambda i: (0, 0), pipeline_mode=pl.Buffered(1))] * 2,
        out_shape=[result] * 2,
        scratch_shapes=[pltpu.VMEM(rows_shape, BF16)] * 4
        + [pltpu.VMEM((token_count, width), F32)]
        + [pltpu.SemaphoreType.DMA((2, tiles, experts))] * 2,
        compiler_params=pltpu.CompilerParams(
            collective_id=1, has_side_effects=True, vmem_limit_bytes=VMEM
        ),
        name="results",
    )(hidden, gates_grad, ups_grad, gate, up, down, all_gate, all_up, all_down, *fixed)


def slots_of(route_ids, home, experts, capacity):
    token_count, top_count = route_ids.shape
    relative = (route_ids.reshape(-1) - home + experts) % experts
    onehot = (relative[:, None] == jnp.arange(experts, dtype=jnp.int32)[None, :]).astype(jnp.int32)
    before = jnp.cumsum(onehot, axis=0) - onehot
    target = relative * capacity + jnp.sum(before * onehot, axis=1)
    return target.reshape(token_count, top_count)


def pickers_of(pair_slot, experts, capacity):
    flat = pair_slot.T.reshape(-1)
    slots = jnp.arange(experts * capacity, dtype=jnp.int32).reshape(experts, 1, capacity)
    return (flat[None, :, None] == slots).astype(BF16)


def inverse_of(values):
    return lax.rsqrt(jnp.mean(values * values, axis=-1, keepdims=True) + EPSILON)


def body(tokens, grad_out, norm_gain, expert_ids, gate_weights, w_gate, w_up, w_down):
    tokens = tokens[0]
    grad_rows = grad_out[0]
    gain = norm_gain[0][None, :]
    route_ids = expert_ids[0]
    route_weights = gate_weights[0]
    token_count, width = tokens.shape
    top_count = route_ids.shape[1]
    devices = lax.axis_size("expert")
    pipes = lax.axis_size("pipe")
    experts = devices // SLICES
    step_size = 4 * experts * SLICES
    capacity = min(
        token_count, SLICES * ((token_count * top_count * 5 + step_size - 1) // step_size)
    )
    home = lax.axis_index("expert") // SLICES
    same = lambda d: d

    gate, up, down = w_gate[0], w_up[0], w_down[0]

    routing = jnp.concatenate([route_ids.astype(F32), route_weights], axis=1)
    routing_next = move(routing, 1, same)
    routing_prev = routing_next if pipes == 2 else move(routing, -1, same)
    gain_prev = move(gain, -1, same)

    values = tokens.astype(F32)
    normed = (values * inverse_of(values) * gain).astype(BF16)
    pair_slot = slots_of(route_ids, home, experts, capacity)
    picker = jnp.any(
        pair_slot[None, :, :]
        == jnp.arange(experts * capacity, dtype=jnp.int32)[:, None, None],
        axis=2,
    ).astype(BF16)

    def slotted(rows):
        return dot_nn(picker, rows).astype(BF16).reshape(experts, capacity, width)

    rows_in, rows_back, all_gate, all_up, all_down, tok_next, tok_prev, grad_prev = gather_all(
        slotted(normed), slotted(grad_rows), gate, up, down, tokens, grad_rows
    )
    rows_in = rows_in.reshape(experts * capacity, width)
    rows_back = rows_back.reshape(experts * capacity, width)

    hidden, gates_grad, ups_grad = [], [], []
    for j in range(SLICES):
        gate_cols, up_cols, down_rows = (
            (gate, up, down) if j == 0 else (all_gate[j - 1], all_up[j - 1], all_down[j - 1])
        )
        gate_pre = dot_nn(rows_in, gate_cols)
        up_pre = dot_nn(rows_in, up_cols)
        sig = jax.nn.sigmoid(gate_pre)
        swish = gate_pre * sig
        hidden.append((swish * up_pre).astype(BF16))
        grad_hidden = dot_nt(rows_back, down_rows)
        gates_grad.append((grad_hidden * up_pre * sig * (1.0 + gate_pre * (1.0 - sig))).astype(BF16))
        ups_grad.append((grad_hidden * swish).astype(BF16))
    hidden = jnp.concatenate(hidden, axis=1)
    gates_grad = jnp.concatenate(gates_grad, axis=1)
    ups_grad = jnp.concatenate(ups_grad, axis=1)

    def routing_of(table):
        ids = table[:, :top_count].astype(jnp.int32)
        slots = slots_of(ids, home, experts, capacity)
        return pickers_of(slots, experts, capacity), table[:, top_count:]

    pick_next, weights_next = routing_of(routing_next)
    pick_prev, weights_prev = routing_of(routing_prev)
    next_rows, prev_rows = results(
        hidden, gates_grad, ups_grad, gate, up, down, all_gate, all_up, all_down,
        tok_next, tok_prev, grad_prev, gain_prev, inverse_of(tok_prev.astype(F32)),
        pick_next, weights_next, pick_prev, weights_prev,
    )
    return (next_rows[None], prev_rows[None])


def solution(mesh):
    return jax.shard_map(
        body,
        mesh=mesh,
        in_specs=(
            P("pipe", "expert", None),
            P("pipe", "expert", None),
            P("pipe", None),
            P("pipe", "expert", None),
            P("pipe", "expert", None),
            P("pipe", None, "expert"),
            P("pipe", None, "expert"),
            P("pipe", "expert", None),
        ),
        out_specs=(P("pipe", "expert", None), P("pipe", "expert", None)),
        check_vma=False,
    )
```

time: 657 us -> 522 us (0.79)
  waiting for transfers between devices: 503 us -> 0.01 us
  Pallas kernels: 24.4 us -> 461 us
  matrix products: 64.7 us -> 30.2 us
  starting transfers between devices: 30.1 us -> 2.08 us
  other arithmetic: 20 us -> 9.78 us
    ppermute x27 -> x2, waiting for transfers between devices: 503 us -> 0.01 us  [move(): return lax.ppermute(value, ('pipe', 'expert'), pairs)]
    pallas_call x2, Pallas kernels: 24.4 us -> 461 us  [the longest x1 246 us: gather_all(): pl.pallas_call(kernel, in_specs=[ANY] * 7, out_specs=[ANY] * 8, out_shape...]
    dot_general x20 -> x10, matrix products: 56.1 us -> 24.5 us  [dot_nn(): return jnp.dot(left_arr, right_arr, preferred_element_type=F32)]
    ppermute x27 -> x2, starting transfers between devices: 30.1 us -> 2.08 us  [move(): return lax.ppermute(value, ('pipe', 'expert'), pairs)]
    concatenate x3 -> x0, other arithmetic: 7.13 us -> none  [the longest x2 7.05 us: dispatch(): return jnp.concatenate(blocks, axis=0)]
  transfers between devices with their start and end apart: 27 -> 2, of which waited for: 14 -> 0; matrix products, arithmetic and copies ran while one was open for 13% -> 8% of each run, Pallas kernels for 4% -> 47%
where the time goes in v2:
time: 522 us; the launch traced here: 519 us
  Pallas kernels  461 us (88%)
  matrix products  30.2 us (6%)
  local copies, waits for them, and re-layouts  14.7 us (3%)
  other arithmetic  9.78 us (2%)
    pallas_call x1, Pallas kernels, gather_all(): pl.pallas_call(kernel, in_specs=[ANY] * 7, out_specs=[ANY] * 8, out_shape...  246 us
    pallas_call x1, Pallas kernels, results(): pl.pallas_call(kernel, grid=(tiles,), in_specs=in_specs, out_specs=[pl.Bl...  215 us
    dot_general x10, matrix products, dot_nn(): return jnp.dot(left_arr, right_arr, preferred_element_type=F32)  24.5 us
    unnamed x52, local copies, waits for them, and re-layouts  11.5 us
  transfers between devices with their start and end apart: 2, of which 0 were waited for; matrix products, arithmetic and copies ran while one was open for 8% of the time, Pallas kernels for 47%

profile of v2, /device:TPU:18, one launch (start us, length us, event | category | flops | bytes accessed | tf_op | source)
XLA Modules:
  0.0 518.6 jit_solution(17359211779456309838)
XLA Ops:
  2.8 1.5 collective-permute-start
  4.7 1.2 reduce-window.14
  6.7 1.9 fusion
  8.6 5.0 convolution_convert_fusion
  13.7 3.6 convolution_convert_fusion.1
  17.3 245.9 %gather_all.1 = (bf16[4,80,7168]{2,1,0:T(8,128)(2,1)}, bf16[4,80,7168]{2,1,0:T(8,128)(2,1)}, bf16[3,7168,256]{2,1,0:T(8,128)(2,1)}, bf16[3,7168,256]{2,1,0:T(8,1...) custom-call(bf16[4,80,7168]{2,1,0:T(8,128)(2,1)} %bitcast.123, ...), custom_call_target="tpu_custom_call" | custom-call | tf_op jit(solution)/shard_map/gather_all/pallas_call | solution.py:115
  263.2 3.8 fusion.60
  268.0 1.3 fusion.62
  271.3 2.1 fusion.17
  273.5 1.4 fusion.13
  275.8 2.1 fusion.19
  278.0 2.1 fusion.15
  280.1 1.4 fusion.9
  281.7 1.5 fusion.11
  284.3 1.4 multiply_convert_fusion.3
  286.3 1.4 slice-done.8
  287.8 1.4 multiply_convert_fusion.2
  289.2 1.4 multiply_convert_fusion.1
  290.7 1.4 multiply_convert_fusion
  293.1 1.2 pad_maximum_fusion
  295.4 1.2 reduce-window.16
  299.4 214.9 %results.1 = (bf16[128,7168]{1,0:T(8,128)(2,1)}, bf16[128,7168]{1,0:T(8,128)(2,1)}) custom-call(bf16[320,1024]{1,0:T(8,128)(2,1)} %get-tuple-element.34.h, bf16[320,1024]{1,0:T(8,128)(2,1)} %get-tuple-element.35.gg, bf16[320,1024]{1,0:T(8,128)(2,1)} %pad_maximum_fusion.2.ug, bf16[7168,256]{1,0:T(8,128)(2,1)} %bitcast.126, bf16[7168,256]{1,0:T(8,128)(2,1)} %bitcast.128, ...), custom_call_target="tpu_custom_call" | custom-call | tf_op jit(solution)/shard_map/results/pallas_call | solution.py:245
  514.4 3.0 copy.63
  517.3 1.2 copy.64
  (101 shorter events, 13.8 us)
Async XLA Ops:
  2.2 292.8 %collective-permute-start.1 = (f32[128,4]{1,0:T(8,128)S(1)}, f32[128,4]{1,0:T(8,128)S(1)}, u32[]{:S(2)}, u32[]{:S(2)}) collective-permute-start(f32[128,4]{1,0:T(8,128)S(1)} %copy.52), channel_id=1, source_target_pairs={{0,16},{1,17},{2,18},{3,19},{4,20},{5,21},{6,22},{7,23},{8,24},{9,... | collective-permute-start | bytes 6152 | tf_op jit(solution)/shard_map/ppermute | solution.py:21
  2.8 296.0 %collective-permute-start = (f32[1,7168]{1,0:T(1,128)}, f32[1,7168]{1,0:T(1,128)S(1)}, u32[]{:S(2)}, u32[]{:S(2)}) collective-permute-start(f32[1,7168]{1,0:T(1,128)} %param.10), channel_id=1, source_target_pairs={{0,16},{1,17},{2,18},{3,19},{4,20},{5,21},{6,22},{7,23},{8,24},{9,... | collective-permute-start | bytes 86024 | tf_op jit(solution)/shard_map/ppermute | solution.py:21
  8.6 5.1 copy-start
  8.6 5.0 copy-start.6
  17.3 245.9 %copy-start.3 = (bf16[1,7168,256]{2,1,0:T(8,128)(2,1)S(1)}, bf16[1,7168,256]{2,1,0:T(8,128)(2,1)}, u32[]{:S(2)}) copy-start(bf16[1,7168,256]{2,1,0:T(8,128)(2,1)} %param.14) | copy-start | bytes 11010052
  263.2 3.8 copy-start.2
  263.2 4.8 copy-start.8
  263.2 6.1 %slice-start.3 = ((s8[11010048]{0:T(1024)(128)(4,1)}), s8[4194304]{0:T(1024)(128)(4,1)S(1)}, s32[]{:S(2)}) async-start(s8[11010048]{0:T(1024)(128)(4,1)} %bitcast.133), calls=%async_computation.3 | async-start | bytes 8388608
  263.2 7.2 %slice-start.4 = ((s8[11010048]{0:T(1024)(128)(4,1)}), s8[4194304]{0:T(1024)(128)(4,1)S(1)}, s32[]{:S(2)}) async-start(s8[11010048]{0:T(1024)(128)(4,1)} %bitcast.133), calls=%async_computation.4 | async-start | bytes 8388608
  268.0 3.4 slice-start.5
  271.3 3.5 slice-start
  271.3 3.6 slice-start.1
  273.5 2.4 slice-start.2
  278.0 3.6 slice-start.11
  278.0 5.8 %slice-start.9 = ((s8[4587520]{0:T(1024)(128)(4,1)}), s8[4194304]{0:T(1024)(128)(4,1)S(1)}, s32[]{:S(2)}) async-start(s8[4587520]{0:T(1024)(128)(4,1)} %bitcast.145), calls=%async_computation.9 | async-start | bytes 8388608
  280.1 1.6 slice-start.12
  280.1 3.6 slice-start.10
  281.7 2.6 copy-start.4
  281.7 4.1 slice-start.6
  281.7 4.6 slice-start.7
  284.3 3.4 slice-start.8
  284.3 3.4 copy-start.10
  284.3 3.4 copy-start.11
  514.4 3.0 copy-start.5
  (3 other events, 3.6 us)

commit v3 on v0

v3 whole, which is shorter than its diff:
```python
import jax
import jax.numpy as jnp
from jax import lax
from jax.experimental import pallas as pl
from jax.experimental.pallas import tpu as pltpu
from jax.sharding import PartitionSpec as P

SLICES = 4
EPSILON = 1e-06
BF16 = jnp.bfloat16
F32 = jnp.float32


def move(value, pipe_steps, expert_map):
    pipes, devices = lax.axis_size("pipe"), lax.axis_size("expert")
    pairs = [
        (p * devices + d, ((p + pipe_steps) % pipes) * devices + expert_map(d))
        for p in range(pipes)
        for d in range(devices)
    ]
    return lax.ppermute(value, ("pipe", "expert"), pairs)


def dot_nt(left_arr, right_arr):
    return lax.dot_general(
        left_arr, right_arr, (((1,), (1,)), ((), ())), preferred_element_type=F32
    )


def dot_nn(left_arr, right_arr):
    return jnp.dot(left_arr, right_arr, preferred_element_type=F32)


def tile_of(width):
    for tile in (1024, 512, 256, 128):
        if width % tile == 0:
            return tile
    return width


MESH = pl.DeviceIdType.MESH
ANY = pl.BlockSpec(memory_space=pl.ANY)


def sections():
    pipe, pipes = lax.axis_index("pipe"), lax.axis_size("pipe")
    return pipe, lax.rem(pipe + 1, pipes), lax.rem(pipe + pipes - 1, pipes)


def greet(partners):
    barrier = pltpu.get_barrier_semaphore()
    for partner in partners:
        pl.semaphore_signal(barrier, inc=1, device_id=partner, device_id_type=MESH)
    pl.semaphore_wait(barrier, len(partners))


VMEM = 60 * 1024 * 1024


def layer(slots_in, slots_grad, gate, up, down, tokens, grad_rows,
          gain_prev, inverse_prev, pick_next, wt_next, pick_prev, wt_prev):
    experts, capacity, width = slots_in.shape
    rows = experts * capacity
    ffd = down.shape[0]
    token_count, top = wt_next.shape
    devices, pipes = lax.axis_size("expert"), lax.axis_size("pipe")
    tile = tile_of(width)
    tiles = width // tile

    def kernel(si, sg, wg, wu, wd, tok, grd, gain, inv, pn, wn, pp, wp,
               next_ref, prev_ref, ag, au, ad,
               ri, rg, tn, tp, gp, recv_o, recv_g, scaled, acc_g, acc_u, acc_h, hid, gg, ug,
               buf_g, buf_u, buf_d,
               far_s, far_r, cross_s, cross_r, near_s, near_r, rows_s, rows_r, tok_s, tok_r,
               load_sem, own_sem, send, recv):
        pipe, after, ahead = sections()
        me = lax.axis_index("expert")
        place = lax.rem(me, SLICES)
        far = me - place + lax.rem(place + 2, SLICES)
        near = me + 1 - 2 * lax.rem(me, 2)
        others = [lax.rem(me + SLICES * s, devices) for s in range(1, experts)]
        homes = [lax.rem(me + devices - SLICES * s, devices) for s in range(experts)]
        greet(
            [(pipe, d) for d in others]
            + [(pipe, far), (pipe, near)]
            + [(p, d) for p in (after, ahead) for d in homes]
        )
        weights = ((wg, ag, buf_g), (wu, au, buf_u), (wd, ad, buf_d))
        stages = (ri, rg)

        def remote(source, target, send_sem, recv_sem, device):
            return pltpu.make_async_remote_copy(
                src_ref=source, dst_ref=target, send_sem=send_sem, recv_sem=recv_sem,
                device_id=device, device_id_type=MESH,
            )

        def cols_of(i):
            return pl.ds(pl.multiple_of(i * tile, tile), tile)

        def part(ref, which, i):
            return ref.at[cols_of(i), :] if which < 2 else ref.at[:, cols_of(i)]

        def far_copy(which, i):
            own, full, _ = weights[which]
            return remote(
                part(own, which, i), part(full.at[1], which, i),
                far_s.at[which, i], far_r.at[which, i], (pipe, far),
            )

        def cross_copy(which, i):
            full = weights[which][1]
            return remote(
                part(full.at[1], which, i), part(full.at[2], which, i),
                cross_s.at[which, i], cross_r.at[which, i], (pipe, near),
            )

        def near_copy(which):
            own, full, _ = weights[which]
            return remote(own, full.at[0], near_s.at[which], near_r.at[which], (pipe, near))

        def row_copy(which, i, s):
            return remote(
                (si, sg)[which].at[s, :, cols_of(i)], stages[which].at[s, :, cols_of(i)],
                rows_s.at[which, i, s - 1], rows_r.at[which, i, s - 1], (pipe, others[s - 1]),
            )

        def own_copy(which):
            return pltpu.make_async_copy((si, sg)[which].at[0], stages[which].at[0], own_sem.at[which])

        def token_copies():
            moves = [(tok, tn, after), (grd, gp, ahead), (tok, tp, ahead)]
            return [
                remote(source, target, tok_s.at[n], tok_r.at[n], (device, me))
                for n, (source, target, device) in enumerate(moves)
            ]

        def loads(which, i):
            own, full, buf = weights[which]
            slot = lax.rem(i, 2)
            return [
                pltpu.make_async_copy(
                    part(own if j == 0 else full.at[j - 1], which, i),
                    buf.at[slot, j],
                    load_sem.at[which, slot, j],
                )
                for j in range(SLICES)
            ]

        def load(kinds, i):
            for which in kinds:
                for copy in loads(which, i):
                    copy.start()

        def loaded(kinds, i):
            for which in kinds:
                for copy in loads(which, i):
                    copy.wait()

        def result_copy(which, i, s):
            return remote(
                stages[which].at[s, :, cols_of(i)], (recv_o, recv_g)[which].at[s, :, cols_of(i)],
                send.at[which, i, s], recv.at[which, i, s], ((after, ahead)[which], homes[s]),
            )

        def ship(which, i, total):
            for s in range(experts):
                stages[which][s, :, cols_of(i)] = total[s * capacity : (s + 1) * capacity].astype(BF16)
            for s in range(experts):
                result_copy(which, i, s).start()

        def send_rows(which, i):
            for s in range(experts - 1, 0, -1):
                row_copy(which, i, s).start()

        def send_far(kinds, i):
            for which in kinds:
                far_copy(which, i).start()

        def tile_rows(which, i):
            return stages[which][:, :, cols_of(i)].reshape(rows, tile)

        def piece(j):
            return slice(j * ffd, (j + 1) * ffd)

        first_far, first_down = min(2, tiles), min(4, tiles)
        for i in range(first_far):
            send_far((0, 1), i)

        @pl.loop(0, tiles)
        def _(i):
            send_rows(0, i)

        for which in range(3):
            near_copy(which).start()
        for which in range(2):
            own_copy(which).start()
        for copy in token_copies():
            copy.start()
        acc_g[...] = jnp.zeros_like(acc_g)
        acc_u[...] = jnp.zeros_like(acc_u)
        acc_h[...] = jnp.zeros_like(acc_h)
        near_copy(0).wait()
        near_copy(1).wait()
        own_copy(0).wait()

        def pipeline(kinds, arrive, compute):
            @pl.loop(0, tiles + 2)
            def _(i):
                @pl.when(i < tiles)
                def _():
                    arrive(i)
                    for which in kinds:
                        far_copy(which, i).wait()
                        cross_copy(which, i).start()

                @pl.when((i >= 1) & (i <= tiles))
                def _():
                    for which in kinds:
                        cross_copy(which, i - 1).wait()
                    load(kinds, i - 1)

                @pl.when(i >= 2)
                def _():
                    loaded(kinds, i - 2)
                    compute(i - 2)

        def arrive_first(i):
            send_rows(1, i)

            @pl.when(i + first_far < tiles)
            def _():
                send_far((0, 1), i + first_far)

            @pl.when(i == tiles - 1)
            def _():
                for n in range(first_down):
                    send_far((2,), n)

        def compute_first(i):
            for s in range(1, experts):
                row_copy(0, i, s).wait()
            slot = lax.rem(i, 2)
            block = tile_rows(0, i)
            for j in range(SLICES):
                acc_g[:, piece(j)] += dot_nn(block, buf_g[slot, j])
                acc_u[:, piece(j)] += dot_nn(block, buf_u[slot, j])

        pipeline((0, 1), arrive_first, compute_first)

        for j in range(SLICES):
            gate_pre = acc_g[:, piece(j)]
            hid[:, piece(j)] = (gate_pre * jax.nn.sigmoid(gate_pre) * acc_u[:, piece(j)]).astype(BF16)
        near_copy(2).wait()
        own_copy(1).wait()

        def arrive_down(i):
            @pl.when(i + first_down < tiles)
            def _():
                send_far((2,), i + first_down)

        def compute_down(i):
            slot = lax.rem(i, 2)
            total = dot_nn(hid[:, piece(0)], buf_d[slot, 0])
            for j in range(1, SLICES):
                total += dot_nn(hid[:, piece(j)], buf_d[slot, j])
            ship(0, i, total)
            for s in range(1, experts):
                row_copy(1, i, s).wait()
            block = tile_rows(1, i)
            for j in range(SLICES):
                acc_h[:, piece(j)] += dot_nt(block, buf_d[slot, j])

        pipeline((2,), arrive_down, compute_down)

        load((0, 1), 0)
        for j in range(SLICES):
            gate_pre, up_pre, grad_hidden = acc_g[:, piece(j)], acc_u[:, piece(j)], acc_h[:, piece(j)]
            sig = jax.nn.sigmoid(gate_pre)
            gg[:, piece(j)] = (grad_hidden * up_pre * sig * (1.0 + gate_pre * (1.0 - sig))).astype(BF16)
            ug[:, piece(j)] = (grad_hidden * (gate_pre * sig)).astype(BF16)

        @pl.loop(0, tiles)
        def _(i):
            @pl.when(i + 1 < tiles)
            def _():
                load((0, 1), i + 1)

            loaded((0, 1), i)
            slot = lax.rem(i, 2)
            total = dot_nt(gg[:, piece(0)], buf_g[slot, 0]) + dot_nt(ug[:, piece(0)], buf_u[slot, 0])
            for j in range(1, SLICES):
                total += dot_nt(gg[:, piece(j)], buf_g[slot, j]) + dot_nt(ug[:, piece(j)], buf_u[slot, j])
            ship(1, i, total)

        def picked(target, pick, scale, cols):
            total = dot_nn(pick[0], target[0, :, cols])
            for s in range(1, experts):
                total += dot_nn(pick[s], target[s, :, cols])
            value = total[:token_count] * scale[:, 0:1]
            for n in range(1, top):
                value += total[n * token_count : (n + 1) * token_count] * scale[:, n : n + 1]
            return value

        for copy in token_copies():
            copy.wait()

        @pl.loop(0, tiles)
        def _(i):
            cols = cols_of(i)
            for s in range(experts):
                result_copy(0, i, s).wait()
            next_ref[:, cols] = (tn[:, cols].astype(F32) + picked(recv_o, pn, wn, cols)).astype(BF16)

        def finish(i, mean):
            cols = cols_of(i)
            for s in range(experts):
                result_copy(1, i, s).wait()
            value = picked(recv_g, pp, wp, cols) * gain[:, cols]
            scaled[:, cols] = value
            return mean + jnp.sum(value * tp[:, cols].astype(F32), axis=1, keepdims=True)

        mean = lax.fori_loop(0, tiles, finish, jnp.zeros((token_count, 1), F32)) / width
        inverse = inv[...]
        factor = inverse * inverse * inverse * mean

        @pl.loop(0, tiles)
        def _(i):
            cols = cols_of(i)
            prev_ref[:, cols] = (
                gp[:, cols].astype(F32) + inverse * scaled[:, cols] - tp[:, cols].astype(F32) * factor
            ).astype(BF16)

    three = lambda value: jax.ShapeDtypeStruct((3,) + value.shape, value.dtype)
    in_vmem = pl.BlockSpec(memory_space=pltpu.VMEM)
    result = jax.ShapeDtypeStruct((token_count, width), BF16)
    row_block = pltpu.VMEM((experts, capacity, width), BF16)
    token_block = pltpu.VMEM((token_count, width), BF16)
    wide = (rows, SLICES * ffd)
    dma = pltpu.SemaphoreType.DMA
    return pl.pallas_call(
        kernel,
        in_specs=[ANY] * 7 + [in_vmem] * 6,
        out_specs=[in_vmem] * 2 + [ANY] * 3,
        out_shape=[result] * 2 + [three(gate), three(up), three(down)],
        scratch_shapes=[row_block] * 2
        + [token_block] * 3
        + [row_block] * 2
        + [pltpu.VMEM((token_count, width), F32)]
        + [pltpu.VMEM(wide, F32)] * 3
        + [pltpu.VMEM(wide, BF16)] * 3
        + [pltpu.VMEM((2, SLICES, tile, ffd), BF16)] * 2
        + [pltpu.VMEM((2, SLICES, ffd, tile), BF16)]
        + [dma((3, tiles))] * 4
        + [dma((3,))] * 2
        + [dma((2, tiles, experts - 1))] * 2
        + [dma((3,))] * 2
        + [dma((3, 2, SLICES)), dma((2,))]
        + [dma((2, tiles, experts))] * 2,
        compiler_params=pltpu.CompilerParams(
            collective_id=0, has_side_effects=True, vmem_limit_bytes=VMEM
        ),
        name="layer",
    )(slots_in, slots_grad, gate, up, down, tokens, grad_rows,
      gain_prev, inverse_prev, pick_next, wt_next, pick_prev, wt_prev)[:2]


def slots_of(route_ids, home, experts, capacity):
    token_count, top_count = route_ids.shape
    relative = (route_ids.reshape(-1) - home + experts) % experts
    onehot = (relative[:, None] == jnp.arange(experts, dtype=jnp.int32)[None, :]).astype(jnp.int32)
    before = jnp.cumsum(onehot, axis=0) - onehot
    target = relative * capacity + jnp.sum(before * onehot, axis=1)
    return target.reshape(token_count, top_count)


def pickers_of(pair_slot, experts, capacity):
    flat = pair_slot.T.reshape(-1)
    slots = jnp.arange(experts * capacity, dtype=jnp.int32).reshape(experts, 1, capacity)
    return (flat[None, :, None] == slots).astype(BF16)


def inverse_of(values):
    return lax.rsqrt(jnp.mean(values * values, axis=-1, keepdims=True) + EPSILON)


def body(tokens, grad_out, norm_gain, expert_ids, gate_weights, w_gate, w_up, w_down):
    tokens = tokens[0]
    grad_rows = grad_out[0]
    gain = norm_gain[0][None, :]
    route_ids = expert_ids[0]
    route_weights = gate_weights[0]
    token_count, width = tokens.shape
    top_count = route_ids.shape[1]
    devices = lax.axis_size("expert")
    pipes = lax.axis_size("pipe")
    experts = devices // SLICES
    step_size = 4 * experts * SLICES
    capacity = min(
        token_count, SLICES * ((token_count * top_count * 5 + step_size - 1) // step_size)
    )
    home = lax.axis_index("expert") // SLICES
    same = lambda d: d

    gate, up, down = w_gate[0], w_up[0], w_down[0]

    values = tokens.astype(F32)
    inverse = inverse_of(values)
    normed = (values * inverse * gain).astype(BF16)
    pair_slot = slots_of(route_ids, home, experts, capacity)
    picker = jnp.any(
        pair_slot[None, :, :]
        == jnp.arange(experts * capacity, dtype=jnp.int32)[:, None, None],
        axis=2,
    ).astype(BF16)

    def slotted(rows):
        return dot_nn(picker, rows).astype(BF16).reshape(experts, capacity, width)

    routing = jnp.concatenate([pair_slot.astype(F32), route_weights, inverse], axis=1)
    routing_next = move(routing, 1, same)
    routing_prev = routing_next if pipes == 2 else move(routing, -1, same)
    gain_prev = move(gain, -1, same)

    def routing_of(table):
        slots = table[:, :top_count].astype(jnp.int32)
        return pickers_of(slots, experts, capacity), table[:, top_count : 2 * top_count]

    pick_next, weights_next = routing_of(routing_next)
    pick_prev, weights_prev = routing_of(routing_prev)
    next_rows, prev_rows = layer(
        slotted(normed), slotted(grad_rows), gate, up, down, tokens, grad_rows,
        gain_prev, routing_prev[:, 2 * top_count :],
        pick_next, weights_next, pick_prev, weights_prev,
    )
    return (next_rows[None], prev_rows[None])


def solution(mesh):
    return jax.shard_map(
        body,
        mesh=mesh,
        in_specs=(
            P("pipe", "expert", None),
            P("pipe", "expert", None),
            P("pipe", None),
            P("pipe", "expert", None),
            P("pipe", "expert", None),
            P("pipe", None, "expert"),
            P("pipe", None, "expert"),
            P("pipe", "expert", None),
        ),
        out_specs=(P("pipe", "expert", None), P("pipe", "expert", None)),
        check_vma=False,
    )
```

time: 1830 us -> 435 us (0.24)
  waiting for transfers between devices: 1590 us -> 0.01 us
  Pallas kernels: 0 us -> 406 us
  matrix products: 84.3 us -> 7 us
  local copies, waits for them, and re-layouts: 64.6 us -> 7.5 us
  other arithmetic: 58.8 us -> 5.81 us
  starting transfers between devices: 24.3 us -> 2.16 us
    all_to_all x4 -> x0, waiting for transfers between devices: 1510 us -> none  [the longest x1 393 us: body(): lax.all_to_all(spread_in, 'expert', split_axis=0, concat_axis=0, tiled=True)]
    pallas_call x0 -> x1, Pallas kernels: none -> 406 us  [layer(): pl.pallas_call(kernel, in_specs=[ANY] * 7 + [in_vmem] * 6, out_specs=[in_...]
    ppermute x2, waiting for transfers between devices: 79 us -> 0.01 us  [move(): return lax.ppermute(value, ('pipe', 'expert'), pairs)]
    dot_general x8 -> x2, matrix products: 84.3 us -> 7 us  [dot_nn(): return jnp.dot(left_arr, right_arr, preferred_element_type=F32)]
    reduce_sum x6 -> x2, other arithmetic: 54.2 us -> 1.96 us  [the longest x1 1.94 us: inverse_of(): jnp.mean(values * values, axis=-1, keepdims=True) + EPSILON]
    gather x4 -> x0, local copies, waits for them, and re-layouts: 43.4 us -> none  [the longest x2 21.7 us: body(): jnp.take(merged_grad, pair_slot, axis=0) * weights]
    all_to_all x4 -> x0, starting transfers between devices: 22.2 us -> none  [the longest x1 6.32 us: body(): lax.all_to_all(spread_in, 'expert', split_axis=0, concat_axis=0, tiled=True)]
  transfers between devices with their start and end apart: 6 -> 2, of which waited for: 6 -> 0; matrix products, arithmetic and copies ran while one was open for 4% -> 4% of each run, Pallas kernels for 0% -> 0%
where the time goes in v3:
time: 435 us; the launch traced here: 430 us
  Pallas kernels  406 us (93%)
  local copies, waits for them, and re-layouts  7.5 us (2%)
  matrix products  7 us (2%)
  other arithmetic  5.81 us (1%)
    pallas_call x1, Pallas kernels, layer(): pl.pallas_call(kernel, in_specs=[ANY] * 7 + [in_vmem] * 6, out_specs=[in_...  406 us
  transfers between devices with their start and end apart: 2, of which 0 were waited for; matrix products, arithmetic and copies ran while one was open for 4% of the time, Pallas kernels for 0%

profile of v3, /device:TPU:18, one launch (start us, length us, event | category | flops | bytes accessed | tf_op | source)
XLA Modules:
  0.0 429.6 jit_solution(12993013529370242939)
XLA Ops:
  0.6 0.6 collective-permute-start
  1.2 0.7 broadcast_subtract_fusion
  1.9 0.1 copy.38
  2.0 0.1 add.83
  2.2 0.1 add.86
  2.3 1.9 fusion
  4.3 0.1 copy.43
  4.4 1.2 reduce-window.6
  5.7 0.1 copy.39
  5.9 0.1 copy.40
  6.1 0.1 reduce_sum.25
  6.3 0.8 copy.42
  7.1 0.1 pad_maximum_fusion
  7.2 1.6 collective-permute-start.1
  8.7 0.1 reduce_sum.23
  9.1 3.4 convolution_convert_fusion
  12.5 3.6 convolution_convert_fusion.1
  16.1 0.7 fusion.24
  16.9 0.8 compare_convert_fusion.pn.pp
  17.7 0.7 slice.23.inv
  18.4 0.6 copy-done.4
  19.0 406.4 %layer.1 = (bf16[128,7168]{1,0:T(8,128)(2,1)}, bf16[128,7168]{1,0:T(8,128)(2,1)}, bf16[3,7168,256]{2,1,0:T(8,128)(2,1)}, bf16[3,7168,256]{2,1,0:T(8,128)(2,1)}, bf16[3,256,7168]{2,1,0:T(8,128)(2,1)}) custom-call(bf16[4,80,7168]{2,1,0:T(8,128)(2,1)} %bitcast.51, bf16[4,80,7168]{2,1,0:T(8,128)(2,1)} %bitcast.50, bf16[7168,256]{1,0:T(8,128)(2,1)} %bitcast.54, ...), custom_call_target="tpu_custom_call" | custom-call | tf_op jit(solution)/shard_map/layer/pallas_call | solution.py:340
  425.4 3.0 copy.49
  428.4 1.2 copy.50
  (27 shorter events, 0.5 us)
Async XLA Ops:
  0.6 8.4 %copy-start.1 = (bf16[1,128,7168]{2,1,0:T(8,128)(2,1)S(1)}, bf16[1,128,7168]{2,1,0:T(8,128)(2,1)}, u32[]{:S(2)}) copy-start(bf16[1,128,7168]{2,1,0:T(8,128)(2,1)} %param.9) | copy-start | bytes 5505028
  0.6 17.8 %collective-permute-start = (f32[1,7168]{1,0:T(1,128)}, f32[1,7168]{1,0:T(1,128)S(1)}, u32[]{:S(2)}, u32[]{:S(2)}) collective-permute-start(f32[1,7168]{1,0:T(1,128)} %param.10), channel_id=1, source_target_pairs={{0,16},{1,17},{2,18},{3,19},{4,20},{5,21},{6,22},{7,23},{8,24},{9,... | collective-permute-start | bytes 86024 | tf_op jit(solution)/shard_map/ppermute | solution.py:21
  7.2 8.9 %collective-permute-start.1 = (f32[128,5]{1,0:T(8,128)S(1)}, f32[128,5]{1,0:T(8,128)S(1)}, u32[]{:S(2)}, u32[]{:S(2)}) collective-permute-start(f32[128,5]{1,0:T(8,128)S(1)} %pad_maximum_fusion), channel_id=1, source_target_pairs={{0,16},{1,17},{2,18},{3,19},{4,20},{5,21},{6,22},{7,23},{8,24},{9,... | collective-permute-start | bytes 7688 | tf_op jit(solution)/shard_map/ppermute | solution.py:21
  9.0 3.4 copy-start
  9.1 3.4 copy-start.3
  18.4 0.6 copy-start.4
  425.4 3.0 copy-start.2

commit v4 on v3

--- a/solution.py
+++ b/solution.py
@@ -54,25 +54,26 @@
     pl.semaphore_wait(barrier, len(partners))
 
 
-VMEM = 60 * 1024 * 1024
-
-
-def layer(slots_in, slots_grad, gate, up, down, tokens, grad_rows,
+VMEM = 62 * 1024 * 1024
+
+
+def layer(picker, inverse, gain, gate, up, down, tokens, grad_rows,
           gain_prev, inverse_prev, pick_next, wt_next, pick_prev, wt_prev):
-    experts, capacity, width = slots_in.shape
-    rows = experts * capacity
+    rows = picker.shape[0]
+    experts, _, capacity = pick_next.shape
+    width = tokens.shape[1]
     ffd = down.shape[0]
     token_count, top = wt_next.shape
     devices, pipes = lax.axis_size("expert"), lax.axis_size("pipe")
     tile = tile_of(width)
     tiles = width // tile
 
-    def kernel(si, sg, wg, wu, wd, tok, grd, gain, inv, pn, wn, pp, wp,
+    def kernel(pick, inv_own, gain_own, wg, wu, wd, tok, grd, gain, inv, pn, wn, pp, wp,
                next_ref, prev_ref, ag, au, ad,
-               ri, rg, tn, tp, gp, recv_o, recv_g, scaled, acc_g, acc_u, acc_h, hid, gg, ug,
+               ri, rg, si, sg, tn, tp, gp, recv_o, recv_g, scaled, acc_g, acc_u, acc_h, hid, gg, ug,
                buf_g, buf_u, buf_d,
                far_s, far_r, cross_s, cross_r, near_s, near_r, rows_s, rows_r, tok_s, tok_r,
-               load_sem, own_sem, send, recv):
+               load_sem, send, recv):
         pipe, after, ahead = sections()
         me = lax.axis_index("expert")
         place = lax.rem(me, SLICES)
@@ -120,12 +121,9 @@
 
         def row_copy(which, i, s):
             return remote(
-                (si, sg)[which].at[s, :, cols_of(i)], stages[which].at[s, :, cols_of(i)],
+                (si, sg)[which].at[s - 1, :, cols_of(i)], stages[which].at[s, :, cols_of(i)],
                 rows_s.at[which, i, s - 1], rows_r.at[which, i, s - 1], (pipe, others[s - 1]),
             )
-
-        def own_copy(which):
-            return pltpu.make_async_copy((si, sg)[which].at[0], stages[which].at[0], own_sem.at[which])
 
         def token_copies():
             moves = [(tok, tn, after), (grd, gp, ahead), (tok, tp, ahead)]
@@ -169,6 +167,12 @@
                 result_copy(which, i, s).start()
 
         def send_rows(which, i):
+            cols = cols_of(i)
+            value = tok[:, cols].astype(F32) * inv_own[...] * gain_own[:, cols] if which == 0 else grd[:, cols]
+            slots = dot_nn(pick[...], value.astype(BF16))
+            stages[which][0, :, cols] = slots[:capacity].astype(BF16)
+            for s in range(1, experts):
+                (si, sg)[which][s - 1, :, cols] = slots[s * capacity : (s + 1) * capacity].astype(BF16)
             for s in range(experts - 1, 0, -1):
                 row_copy(which, i, s).start()
 
@@ -192,8 +196,6 @@
 
         for which in range(3):
             near_copy(which).start()
-        for which in range(2):
-            own_copy(which).start()
         for copy in token_copies():
             copy.start()
         acc_g[...] = jnp.zeros_like(acc_g)
@@ -201,7 +203,6 @@
         acc_h[...] = jnp.zeros_like(acc_h)
         near_copy(0).wait()
         near_copy(1).wait()
-        own_copy(0).wait()
 
         def pipeline(kinds, arrive, compute):
             @pl.loop(0, tiles + 2)
@@ -251,7 +252,6 @@
             gate_pre = acc_g[:, piece(j)]
             hid[:, piece(j)] = (gate_pre * jax.nn.sigmoid(gate_pre) * acc_u[:, piece(j)]).astype(BF16)
         near_copy(2).wait()
-        own_copy(1).wait()
 
         def arrive_down(i):
             @pl.when(i + first_down < tiles)
@@ -339,10 +339,11 @@
     dma = pltpu.SemaphoreType.DMA
     return pl.pallas_call(
         kernel,
-        in_specs=[ANY] * 7 + [in_vmem] * 6,
+        in_specs=[in_vmem] * 3 + [ANY] * 3 + [in_vmem] * 8,
         out_specs=[in_vmem] * 2 + [ANY] * 3,
         out_shape=[result] * 2 + [three(gate), three(up), three(down)],
         scratch_shapes=[row_block] * 2
+        + [pltpu.VMEM((experts - 1, capacity, width), BF16)] * 2
         + [token_block] * 3
         + [row_block] * 2
         + [pltpu.VMEM((token_count, width), F32)]
@@ -354,13 +355,13 @@
         + [dma((3,))] * 2
         + [dma((2, tiles, experts - 1))] * 2
         + [dma((3,))] * 2
-        + [dma((3, 2, SLICES)), dma((2,))]
+        + [dma((3, 2, SLICES))]
         + [dma((2, tiles, experts))] * 2,
         compiler_params=pltpu.CompilerParams(
             collective_id=0, has_side_effects=True, vmem_limit_bytes=VMEM
         ),
         name="layer",
-    )(slots_in, slots_grad, gate, up, down, tokens, grad_rows,
+    )(picker, inverse, gain, gate, up, down, tokens, grad_rows,
       gain_prev, inverse_prev, pick_next, wt_next, pick_prev, wt_prev)[:2]
 
 
@@ -405,7 +406,6 @@
 
     values = tokens.astype(F32)
     inverse = inverse_of(values)
-    normed = (values * inverse * gain).astype(BF16)
     pair_slot = slots_of(route_ids, home, experts, capacity)
     picker = jnp.any(
         pair_slot[None, :, :]
@@ -413,9 +413,6 @@
         axis=2,
     ).astype(BF16)
 
-    def slotted(rows):
-        return dot_nn(picker, rows).astype(BF16).reshape(experts, capacity, width)
-
     routing = jnp.concatenate([pair_slot.astype(F32), route_weights, inverse], axis=1)
     routing_next = move(routing, 1, same)
     routing_prev = routing_next if pipes == 2 else move(routing, -1, same)
@@ -428,7 +425,7 @@
     pick_next, weights_next = routing_of(routing_next)
     pick_prev, weights_prev = routing_of(routing_prev)
     next_rows, prev_rows = layer(
-        slotted(normed), slotted(grad_rows), gate, up, down, tokens, grad_rows,
+        picker, inverse, gain, gate, up, down, tokens, grad_rows,
         gain_prev, routing_prev[:, 2 * top_count :],
         pick_next, weights_next, pick_prev, weights_prev,
     )

time: 435 us -> 431 us (level)
  matrix products: 7 us -> 0 us
  Pallas kernels: 406 us -> 411 us
    dot_general x2 -> x0, matrix products: 7 us -> none  [dot_nn(): return jnp.dot(left_arr, right_arr, preferred_element_type=F32)]
    pallas_call x1, Pallas kernels: 406 us -> 411 us  [layer(): pl.pallas_call(kernel, in_specs=[in_vmem] * 3 + [ANY] * 3 + [in_vmem] * 8...]
  transfers between devices with their start and end apart: 2 -> 2, of which waited for: 0 -> 1; matrix products, arithmetic and copies ran while one was open for 4% -> 2% of each run, Pallas kernels for 0% -> 0%
where the time goes in v4:
time: 431 us; the launch traced here: 430 us
  Pallas kernels  411 us (95%)
  local copies, waits for them, and re-layouts  7.47 us (2%)
  other arithmetic  6.46 us (1%)
    pallas_call x1, Pallas kernels, layer(): pl.pallas_call(kernel, in_specs=[in_vmem] * 3 + [ANY] * 3 + [in_vmem] * 8...  411 us
  transfers between devices with their start and end apart: 2, of which 1 were waited for; matrix products, arithmetic and copies ran while one was open for 2% of the time, Pallas kernels for 0%

profile of v4, /device:TPU:18, one launch (start us, length us, event | category | flops | bytes accessed | tf_op | source)
XLA Modules:
  0.0 430.0 jit_solution(12530971396231052917)
XLA Ops:
  0.6 0.6 collective-permute-start
  1.2 0.7 broadcast_subtract_fusion
  1.9 0.1 copy.42
  2.0 0.1 add.82
  2.2 0.1 add.85
  2.3 1.9 multiply_reduce_fusion
  4.3 0.1 copy.49.inv_own
  4.4 1.2 reduce-window.6
  5.7 0.1 copy.43
  5.9 0.1 copy.44
  6.1 0.1 reduce_sum.25
  6.3 0.8 copy.46
  7.1 0.1 pad_maximum_fusion
  7.2 1.6 collective-permute-start.1
  8.7 0.1 reduce_sum.23
  9.0 0.7 convert_element_type.26.pick
  9.7 1.8 collective-permute-done.1
  11.5 0.7 fusion.15
  12.3 0.8 compare_convert_fusion.pn.pp
  13.1 0.7 slice.23.inv
  13.8 0.6 copy-done.2
  14.4 411.3 %layer.1 = (bf16[128,7168]{1,0:T(8,128)(2,1)}, bf16[128,7168]{1,0:T(8,128)(2,1)}, bf16[3,7168,256]{2,1,0:T(8,128)(2,1)}, bf16[3,7168,256]{2,1,0:T(8,128)(2,1)}, bf16[3,256,7168]{2,1,0:T(8,128)(2,1)}) custom-call(bf16[320,128]{1,0:T(8,128)(2,1)} %convert_element_type.26.pick, f32[128,1]{1,0:T(8,128)} %copy-done.1, f32[1,7168]{1,0:T(1,128)} %gain_own.1, ...), custom_call_target="tpu_custom_call" | custom-call | tf_op jit(solution)/shard_map/layer/pallas_call | solution.py:340
  425.7 3.0 copy.54
  428.7 1.2 copy.55
  (22 shorter events, 0.5 us)
Async XLA Ops:
  0.6 13.2 %collective-permute-start = (f32[1,7168]{1,0:T(1,128)}, f32[1,7168]{1,0:T(1,128)S(1)}, u32[]{:S(2)}, u32[]{:S(2)}) collective-permute-start(f32[1,7168]{1,0:T(1,128)} %gain_own.1), channel_id=1, source_target_pairs={{0,16},{1,17},{2,18},{3,19},{4,20},{5,21},{6,22},{7,23},{8,24},{9,... | collective-permute-start | bytes 86024 | tf_op jit(solution)/shard_map/ppermute | solution.py:21
  4.4 9.4 %copy-start.1 = (f32[128,1]{1,0:T(8,128)}, f32[128,1]{1,0:T(8,128)S(1)}, u32[]{:S(2)}) copy-start(f32[128,1]{1,0:T(8,128)S(1)} %copy.49.inv_own) | copy-start | bytes 1540
  7.2 4.3 %collective-permute-start.1 = (f32[128,5]{1,0:T(8,128)S(1)}, f32[128,5]{1,0:T(8,128)S(1)}, u32[]{:S(2)}, u32[]{:S(2)}) collective-permute-start(f32[128,5]{1,0:T(8,128)S(1)} %pad_maximum_fusion), channel_id=1, source_target_pairs={{0,16},{1,17},{2,18},{3,19},{4,20},{5,21},{6,22},{7,23},{8,24},{9,... | collective-permute-start | bytes 7688 | tf_op jit(solution)/shard_map/ppermute | solution.py:21
  13.8 0.6 copy-start.2
  425.7 3.0 copy-start
